TPU v7x, 256 devices: a whole 4x4x8 slice. The times are simulated.
256 devices in a mesh: span: 4 (over y), ty: 8 (over z_hi, core), tx: 8 (over z_lo, x).
Axes of the slice: x: 4, y: 4, z: 8 (z_hi: 4, z_lo: 2; z = z_hi * 2 + z_lo), core: 2. Of those that a mesh axis runs over, the one named last changes fastest.
Arguments:
- queries: bfloat16 [4, 8, 8, 128, 1536], P('span', 'ty', 'tx'), may hold values from -125 to 125
- key_value: bfloat16 [4, 8, 8, 128, 1024], P('span', 'ty', 'tx'), may hold values from -5 to 5
- pattern: int32 [4, 8, 8, 5], P('span', 'ty', 'tx'), may hold values from 0 to 1
- counts: int32 [4, 8, 8], replicated, may hold values from 64 to 128, as said below
- span_mask: int32 [4, 4], replicated, may hold values from 0 to 1, as said below
Outputs:
- attended: bfloat16 [4, 8, 8, 128, 1536], P('span', 'ty', 'tx')
Inputs may be any that keep to these rules, and one draw needn't show every extreme that they name: `counts`: in every span some tile has all 128 slots valid. span_mask[c, c] is 1 and span_mask[c, c'] is 0 for c' > c.
All inputs are finite; a program needn't handle non-finite values.
Results may differ from a plain program's by a relative error of at most 0.006.
Values may be sent and summed in bfloat16 or wider, within the bound.
A program may use at most 64 MiB of HBM per device.

v0:
```python
import jax
import jax.numpy as jnp
from jax import lax
from jax.sharding import PartitionSpec as P

HEAD_SIZE = 128
NEIGH = 5


def padded(block, sides, width):
    for axis, dim in sides:
        count = lax.axis_size(axis)
        forward = [(i, i + 1) for i in range(count - 1)]
        backward = [(target, source) for source, target in forward]
        low = lax.ppermute(
            lax.slice_in_dim(block, block.shape[dim] - width, None, axis=dim), axis, forward
        )
        high = lax.ppermute(lax.slice_in_dim(block, 0, width, axis=dim), axis, backward)
        block = jnp.concatenate([low, block, high], axis=dim)
    return block


def cross_tiles(extended):
    return jnp.stack(
        [
            extended[:, 1, 1],
            extended[:, 0, 1],
            extended[:, 2, 1],
            extended[:, 1, 0],
            extended[:, 1, 2],
        ],
        axis=1,
    )


def shards(queries, key_value, pattern, counts, span_mask):
    tok_rows = queries.shape[3]
    kv_width = key_value.shape[4] // 2
    kv_heads = kv_width // HEAD_SIZE
    groups = queries.shape[4] // kv_width
    scale = HEAD_SIZE ** (-0.5)
    my_span = lax.axis_index("span")
    my_row = lax.axis_index("ty")
    my_col = lax.axis_index("tx")
    zero_index = jnp.asarray(0).astype(jnp.int32)
    padded_counts = jnp.pad(counts, ((0, 0), (1, 1), (1, 1)))
    window = lax.dynamic_slice(padded_counts, (zero_index, my_row, my_col), (counts.shape[0], 3, 3))
    near_counts = cross_tiles(window)
    own_count = lax.dynamic_index_in_dim(window[:, 1, 1], my_span, 0, keepdims=False)
    allowed = pattern.reshape(NEIGH) > 0
    span_row = lax.dynamic_index_in_dim(span_mask, my_span, 0, keepdims=False) > 0
    query_rows = queries.reshape(tok_rows, kv_heads, groups, HEAD_SIZE)
    row_ids = jnp.arange(tok_rows, dtype=jnp.int32)
    initial = (
        jnp.full((tok_rows, kv_heads, groups), -1e30, jnp.float32),
        jnp.zeros((tok_rows, kv_heads, groups), jnp.float32),
        jnp.zeros((tok_rows, kv_heads, groups, HEAD_SIZE), jnp.float32),
    )
    cached = lax.all_gather(key_value, "span", axis=0, tiled=True)
    extended = padded(cached, (("ty", 1), ("tx", 2)), 1)
    state_now = initial
    kv_piece = cross_tiles(extended)
    for offset in range(kv_piece.shape[0]):
        key_value_block = kv_piece[offset]
        source_span = 0 + offset
        attend_run_max, attend_run_sum, attend_accumulated = state_now
        key_matrix = key_value_block[:, :, :kv_width].reshape(-1, kv_heads, HEAD_SIZE)
        value_rows = key_value_block[:, :, kv_width:].reshape(-1, kv_heads, HEAD_SIZE)
        near_count = lax.dynamic_index_in_dim(near_counts, source_span, 0, keepdims=False)
        open_span = lax.dynamic_index_in_dim(span_row, source_span, 0, keepdims=False)
        live_keys = (
            (row_ids[None, :] < near_count[:, None]) & allowed[:, None] & open_span
        ).reshape(-1)
        scores = (
            jnp.einsum("tkgd,lkd->tkgl", query_rows, key_matrix, preferred_element_type=jnp.float32)
            * scale
        )
        scores = jnp.where(live_keys, scores, -1e30)
        new_max = jnp.maximum(attend_run_max, jnp.max(scores, axis=-1))
        weights = jnp.where(live_keys, jnp.exp(scores - new_max[..., None]), 0.0)
        fade_factor = jnp.exp(attend_run_max - new_max)
        attend_run_sum = attend_run_sum * fade_factor + jnp.sum(weights, axis=-1)
        update = jnp.einsum(
            "tkgl,lkd->tkgd",
            weights.astype(jnp.bfloat16),
            value_rows,
            preferred_element_type=jnp.float32,
        )
        attend_accumulated = attend_accumulated * fade_factor[..., None] + update
        final_output = (new_max, attend_run_sum, attend_accumulated)
        state_now = final_output
    run_max, run_sum, accumulated = state_now
    attended = jnp.where(
        row_ids[:, None, None, None] < own_count, accumulated / run_sum[..., None], 0.0
    )
    return attended.reshape(1, 1, 1, tok_rows, -1).astype(jnp.bfloat16)


def solution(mesh):
    return jax.shard_map(
        shards,
        mesh=mesh,
        in_specs=(
            P("span", "ty", "tx", None, None),
            P("span", "ty", "tx", None, None),
            P("span", "ty", "tx", None),
            P(),
            P(),
        ),
        out_specs=P("span", "ty", "tx", None, None),
        check_vma=False,
    )
```

profile of v0, /device:TPU:95, one launch (start us, length us, event | category | flops | bytes accessed | tf_op | source)
XLA Modules:
  0.0 191.1 jit_solution(15995230202677580363)
XLA Ops:
  7.3 28.2 %all-gather.2.cloned.1.call-done = bf16[4,1,1,128,1024]{4,3,2,1,0:T(8,128)(2,1)} async-done(((bf16[1,1,1,128,1024]{4,3,2,1,0:T(8,128)(2,1)}), bf16[4,1,1,128,1024]{4,3,2,1,0:T(8,128)(2,1)}) %all-gather.2.cloned.1.call-update) | async-done | bytes 1048592 | tf_op jit(solution)/shard_map/all_gather | solution.py:59
  35.5 3.7 %collective-permute-start.1 = (bf16[4,1,1,128,1024]{4,3,0,2,1:T(8,128)(2,1)}, bf16[4,1,1,128,1024]{4,3,0,2,1:T(8,128)(2,1)S(1)}, u32[]{:S(2)}, u32[]{:S(2)}) collective-permute-start(bf16[4,1,1,128,1024]{4,3,0,2,1:T(8,128)(2,1)} %bitcast.168), channel_id=1, source_target_pairs={{8,0},{16,8},{24,16},{32,24},{40,32},{48,40},{56,48},{9,1},{17,9},... | collective-permute-start | bytes 3145736 | tf_op jit(solution)/shard_map/ppermute | solution.py:18
  39.2 5.3 %collective-permute-start = (bf16[4,1,1,128,1024]{4,3,0,2,1:T(8,128)(2,1)}, bf16[4,1,1,128,1024]{4,3,0,2,1:T(8,128)(2,1)S(1)}, u32[]{:S(2)}, u32[]{:S(2)}) collective-permute-start(bf16[4,1,1,128,1024]{4,3,0,2,1:T(8,128)(2,1)} %bitcast.169), channel_id=1, source_target_pairs={{0,8},{8,16},{16,24},{24,32},{32,40},{40,48},{48,56},{1,9},{9,17},... | collective-permute-start | bytes 3145736 | tf_op jit(solution)/shard_map/ppermute | solution.py:15
  44.5 22.0 %collective-permute-done.1 = bf16[4,1,1,128,1024]{4,3,0,2,1:T(8,128)(2,1)S(1)} collective-permute-done((bf16[4,1,1,128,1024]{4,3,0,2,1:T(8,128)(2,1)}, bf16[4,1,1,128,1024]{4,3,0,2,1:T(8,128)(2,1)S(1)}, u32[]{:S(2)}, u32[]{:S(2)}) %collective-permute-start.1) | collective-permute-done | bytes 1048608 | tf_op jit(solution)/shard_map/ppermute | solution.py:18
  66.5 1.2 collective-permute-done
  67.8 1.9 %pad_maximum_fusion = bf16[4,3,1,128,1024]{4,3,2,1,0:T(8,128)(2,1)S(1)} fusion(bf16[4,1,1,128,1024]{4,3,2,1,0:T(8,128)(2,1)S(1)} %bitcast.170, bf16[4,1,1,128,1024]{4,3,2,1,0:T(8,128)(2,1)} %all-gather.2.cloned.1.call-done, bf16[4,1,1,128,1024]{4,3,2,1,0:T(8,128)(2,1)S(1)} %bitcast.171), kind=kLoop, calls=%fused_computation.20 | loop fusion | flops 3145728 | bytes 6291456 | tf_op jit(solution)/shard_map/concatenate | solution.py:19
  69.7 2.2 %copy.51 = bf16[4,3,1,128,1024]{4,3,0,2,1:T(8,128)(2,1)} copy(bf16[4,3,1,128,1024]{4,3,2,1,0:T(8,128)(2,1)S(1)} %pad_maximum_fusion) | data formatting | bytes 6291456 | tf_op jit(solution)/shard_map/concatenate | solution.py:19
  72.0 1.9 collective-permute-start.2
  73.9 3.4 %collective-permute-start.3 = (bf16[4,3,1,128,1024]{4,3,2,1,0:T(8,128)(2,1)S(1)}, bf16[4,3,1,128,1024]{4,3,2,1,0:T(8,128)(2,1)}, u32[]{:S(2)}, u32[]{:S(2)}) collective-permute-start(bf16[4,3,1,128,1024]{4,3,2,1,0:T(8,128)(2,1)S(1)} %pad_maximum_fusion), channel_id=1, source_target_pairs={{1,0},{2,1},{3,2},{4,3},{5,4},{6,5},{7,6},{9,8},{10,9},{11,10},{12... | collective-permute-start | bytes 9437192 | tf_op jit(solution)/shard_map/ppermute | solution.py:18
  77.3 1.2 copy.52
  81.0 1.3 iota_compare_fusion.4
  84.5 2.7 %fusion.93 = (pred[640]{0:T(1024)(128)(4,1)S(1)}, pred[640]{0:T(1024)(128)(4,1)S(1)}, pred[640]{0:T(1024)(128)(4,1)S(1)}, pred[640]{0:T(1024)(128)(4,1)S(1)}) fusion(s32[5]{0:T(128)S(1)} %get-tuple-element.12, pred[]{:T(512)} %bitcast.19, pred[5]{0:T(512)(128)(4,1)S(1)} %compare_bitcast_fusion, pred[]{:T(512)} %bitcast.26, s32[5]{0:T(128)S(1)} %get-tuple-element.11, ...), kind=kLoop, calls=%fused_computation.103 | loop fusion | flops 7680 | bytes 2649 | tf_op jit(solution)/shard_map/and | solution.py:72
  87.2 1.3 bitcast_dynamic-update-slice_fusion.2
  88.5 1.3 bitcast_dynamic-update-slice_fusion.1
  89.9 50.6 %collective-permute-done.2 = bf16[4,3,1,128,1024]{4,3,0,2,1:T(8,128)(2,1)} collective-permute-done((bf16[4,3,1,128,1024]{4,3,0,2,1:T(8,128)(2,1)}, bf16[4,3,1,128,1024]{4,3,0,2,1:T(8,128)(2,1)}, u32[]{:S(2)}, u32[]{:S(2)}) %collective-permute-start.2) | collective-permute-done | bytes 3145760 | tf_op jit(solution)/shard_map/ppermute | solution.py:15
  140.5 1.3 fusion.66
  141.8 4.3 %collective-permute-done.3 = bf16[4,3,1,128,1024]{4,3,2,1,0:T(8,128)(2,1)} collective-permute-done((bf16[4,3,1,128,1024]{4,3,2,1,0:T(8,128)(2,1)S(1)}, bf16[4,3,1,128,1024]{4,3,2,1,0:T(8,128)(2,1)}, u32[]{:S(2)}, u32[]{:S(2)}) %collective-permute-start.3) | collective-permute-done | bytes 3145760 | tf_op jit(solution)/shard_map/ppermute | solution.py:18
  146.1 1.3 fusion.65
  147.4 1.6 slice_bitcast_fusion.2
  150.2 2.3 %reshape.186 = bf16[640,4,128]{2,1,0:T(4,128)(2,1)} reshape(bf16[5,128,512]{2,1,0:T(8,128)(2,1)} %get-tuple-element.29) | data formatting | bytes 1310720 | tf_op jit(solution)/shard_map/reshape | solution.py:68
  152.6 2.3 %reshape.185 = bf16[640,4,128]{2,1,0:T(4,128)(2,1)} reshape(bf16[5,128,512]{2,1,0:T(8,128)(2,1)} %get-tuple-element.30) | data formatting | bytes 1310720 | tf_op jit(solution)/shard_map/reshape | solution.py:67
  154.9 2.4 %fusion.121 = (bf16[5,128,512]{2,1,0:T(8,128)(2,1)}, bf16[5,128,512]{2,1,0:T(8,128)(2,1)}) fusion(bf16[5,128,1024]{2,1,0:T(8,128)(2,1)} %get-tuple-element.22), kind=kLoop, calls=%fused_computation.133 | loop fusion | bytes 2621440 | tf_op jit(solution)/shard_map/slice | solution.py:68
  157.4 2.3 %reshape.190 = bf16[640,4,128]{2,1,0:T(4,128)(2,1)} reshape(bf16[5,128,512]{2,1,0:T(8,128)(2,1)} %get-tuple-element.25) | data formatting | bytes 1310720 | tf_op jit(solution)/shard_map/reshape | solution.py:68
  159.7 2.3 %reshape.189 = bf16[640,4,128]{2,1,0:T(4,128)(2,1)} reshape(bf16[5,128,512]{2,1,0:T(8,128)(2,1)} %get-tuple-element.26) | data formatting | bytes 1310720 | tf_op jit(solution)/shard_map/reshape | solution.py:67
  163.2 2.3 %reshape.188 = bf16[640,4,128]{2,1,0:T(4,128)(2,1)} reshape(bf16[5,128,512]{2,1,0:T(8,128)(2,1)} %get-tuple-element.27) | data formatting | bytes 1310720 | tf_op jit(solution)/shard_map/reshape | solution.py:68
  165.5 2.3 %reshape.187 = bf16[640,4,128]{2,1,0:T(4,128)(2,1)} reshape(bf16[5,128,512]{2,1,0:T(8,128)(2,1)} %get-tuple-element.28) | data formatting | bytes 1310720 | tf_op jit(solution)/shard_map/reshape | solution.py:67
  172.4 2.5 %fusion.8 = (f32[128,4,3]{0,2,1:T(4,128)S(1)}, f32[128,4,3]{0,2,1:T(4,128)S(1)}) fusion(f32[4,640,128,3]{2,1,3,0:T(8,128)S(1)} %get-tuple-element.50, f32[128,4,3]{0,2,1:T(4,128)S(1)} %get-tuple-element.34, pred[640]{0:T(1024)(128)(4,1)S(1)} %get-tuple-element.38, f32[128,4,3]{0,2,1:T(4,128)S(1)} %get-tuple-element.20, ...), kind=kLoop, calls=%fused_computation.21 | loop fusion | flops 9827328 | bytes 7890176 | tf_op jit(solution)/shard_map/reduce_sum | solution.py:82
  175.0 2.7 %fusion.12 = (f32[128,4,3]{0,2,1:T(4,128)S(1)}, f32[128,4,3]{0,2,1:T(4,128)S(1)}) fusion(f32[4,640,128,3]{2,1,3,0:T(8,128)S(1)} %get-tuple-element.46, f32[128,4,3]{0,2,1:T(4,128)S(1)} %get-tuple-element.19, pred[640]{0:T(1024)(128)(4,1)S(1)} %get-tuple-element.36, f32[128,4,3]{0,2,1:T(4,128)S(1)} %get-tuple-element.18, ...), kind=kLoop, calls=%fused_computation.25 | loop fusion | flops 9827328 | bytes 7890176 | tf_op jit(solution)/shard_map/reduce_sum | solution.py:82
  177.8 1.4 fusion.56
  179.1 1.4 fusion.59
  180.5 1.4 fusion.62
  181.9 1.4 fusion.73
  (46 shorter events, 13.4 us)
Async XLA Ops:
  6.5 29.0 %all-gather.2.cloned.1.call-start = ((), (), s32[]{:S(2)}) async-start(), calls=%async_computation | async-start | bytes 1310720 | tf_op jit(solution)/shard_map/all_gather | solution.py:59
  35.5 31.0 %collective-permute-start.1 = (bf16[4,1,1,128,1024]{4,3,0,2,1:T(8,128)(2,1)}, bf16[4,1,1,128,1024]{4,3,0,2,1:T(8,128)(2,1)S(1)}, u32[]{:S(2)}, u32[]{:S(2)}) collective-permute-start(bf16[4,1,1,128,1024]{4,3,0,2,1:T(8,128)(2,1)} %bitcast.168), channel_id=1, source_target_pairs={{8,0},{16,8},{24,16},{32,24},{40,32},{48,40},{56,48},{9,1},{17,9},... | collective-permute-start | bytes 3145736 | tf_op jit(solution)/shard_map/ppermute | solution.py:18
  39.2 28.5 %collective-permute-start = (bf16[4,1,1,128,1024]{4,3,0,2,1:T(8,128)(2,1)}, bf16[4,1,1,128,1024]{4,3,0,2,1:T(8,128)(2,1)S(1)}, u32[]{:S(2)}, u32[]{:S(2)}) collective-permute-start(bf16[4,1,1,128,1024]{4,3,0,2,1:T(8,128)(2,1)} %bitcast.169), channel_id=1, source_target_pairs={{0,8},{8,16},{16,24},{24,32},{32,40},{40,48},{48,56},{1,9},{9,17},... | collective-permute-start | bytes 3145736 | tf_op jit(solution)/shard_map/ppermute | solution.py:15
  66.5 5.4 %copy-start = (bf16[4,1,1,128,1024]{4,3,0,2,1:T(8,128)(2,1)}, bf16[4,1,1,128,1024]{4,3,0,2,1:T(8,128)(2,1)S(1)}, u32[]{:S(2)}) copy-start(bf16[4,1,1,128,1024]{4,3,0,2,1:T(8,128)(2,1)S(1)} %collective-permute-done.1) | copy-start | bytes 3145732
  67.8 4.2 %copy-start.2 = (bf16[4,1,1,128,1024]{4,3,0,2,1:T(8,128)(2,1)}, bf16[4,1,1,128,1024]{4,3,0,2,1:T(8,128)(2,1)S(1)}, u32[]{:S(2)}) copy-start(bf16[4,1,1,128,1024]{4,3,0,2,1:T(8,128)(2,1)S(1)} %collective-permute-done) | copy-start | bytes 3145732
  69.7 8.8 %copy-start.10 = (s32[4,8,8]{2,1,0:T(8,128)S(1)}, s32[4,8,8]{2,1,0:T(8,128)}, u32[]{:S(2)}) copy-start(s32[4,8,8]{2,1,0:T(8,128)} %param.8) | copy-start | bytes 3076
  72.0 68.5 %collective-permute-start.2 = (bf16[4,3,1,128,1024]{4,3,0,2,1:T(8,128)(2,1)}, bf16[4,3,1,128,1024]{4,3,0,2,1:T(8,128)(2,1)}, u32[]{:S(2)}, u32[]{:S(2)}) collective-permute-start(bf16[4,3,1,128,1024]{4,3,0,2,1:T(8,128)(2,1)} %copy.51), channel_id=1, source_target_pairs={{0,1},{1,2},{2,3},{3,4},{4,5},{5,6},{6,7},{8,9},{9,10},{10,11},{11... | collective-permute-start | bytes 9437192 | tf_op jit(solution)/shard_map/ppermute | solution.py:15
  73.9 72.2 %collective-permute-start.3 = (bf16[4,3,1,128,1024]{4,3,2,1,0:T(8,128)(2,1)S(1)}, bf16[4,3,1,128,1024]{4,3,2,1,0:T(8,128)(2,1)}, u32[]{:S(2)}, u32[]{:S(2)}) collective-permute-start(bf16[4,3,1,128,1024]{4,3,2,1,0:T(8,128)(2,1)S(1)} %pad_maximum_fusion), channel_id=1, source_target_pairs={{1,0},{2,1},{3,2},{4,3},{5,4},{6,5},{7,6},{9,8},{10,9},{11,10},{12... | collective-permute-start | bytes 9437192 | tf_op jit(solution)/shard_map/ppermute | solution.py:18
  81.0 8.8 %copy-start.1 = (bf16[4,1,1,128,1024]{4,3,0,2,1:T(8,128)(2,1)S(1)}, bf16[4,1,1,128,1024]{4,3,0,2,1:T(8,128)(2,1)}, u32[]{:S(2)}) copy-start(bf16[4,1,1,128,1024]{4,3,0,2,1:T(8,128)(2,1)} %copy-done) | copy-start | bytes 3145732
  168.0 2.0 %copy-start.5 = (bf16[640,4,128]{2,1,0:T(4,128)(2,1)S(1)}, bf16[640,4,128]{2,1,0:T(4,128)(2,1)}, u32[]{:S(2)}) copy-start(bf16[640,4,128]{2,1,0:T(4,128)(2,1)} %reshape.187) | copy-start | bytes 1966084
  169.1 1.6 copy-start.4
  170.0 1.6 copy-start.3
  175.0 2.8 %copy-start.9 = (bf16[640,4,128]{2,1,0:T(4,128)(2,1)S(1)}, bf16[640,4,128]{2,1,0:T(4,128)(2,1)}, u32[]{:S(2)}) copy-start(bf16[640,4,128]{2,1,0:T(4,128)(2,1)} %reshape.184) | copy-start | bytes 1966084
  177.7 1.4 copy-start.7
  179.1 1.4 copy-start.8
  180.5 1.4 copy-start.6
  180.5 1.4 copy-start.11
Sparse Core Ops, SparseCore 0:
  9.2 26.2 all-gather.1
where the time goes:
time: 195 us; the launch traced here: 191 us
  waiting for transfers between devices  107 us (55%)
  local copies, waits for them, and re-layouts  34.7 us (18%)
  starting transfers between devices  14.3 us (7%)
  between operations  13.7 us (7%)
  other arithmetic  12.6 us (6%)
  matrix products  8.64 us (4%)
    ppermute x2, waiting for transfers between devices, padded(): lax.ppermute(lax.slice_in_dim(block, block.shape[dim] - width, None, axis...  51.8 us
    all_gather x1, waiting for transfers between devices, shards(): cached = lax.all_gather(key_value, 'span', axis=0, tiled=True)  28.2 us
    ppermute x2, waiting for transfers between devices, padded(): lax.ppermute(lax.slice_in_dim(block, 0, width, axis=dim), axis, backward)  26.3 us
    reshape x4, local copies, waits for them, and re-layouts, shards(): key_value_block[:, :, kv_width:].reshape(-1, kv_heads, HEAD_SIZE)  7.99 us
    ppermute x2, starting transfers between devices, padded(): lax.ppermute(lax.slice_in_dim(block, block.shape[dim] - width, None, axis...  7.19 us
    reshape x4, local copies, waits for them, and re-layouts, shards(): key_value_block[:, :, :kv_width].reshape(-1, kv_heads, HEAD_SIZE)  7.14 us
    ppermute x2, starting transfers between devices, padded(): lax.ppermute(lax.slice_in_dim(block, 0, width, axis=dim), axis, backward)  7.1 us
    dot_general x4, matrix products, shards(): jnp.einsum('tkgl,lkd->tkgd', weights.astype(jnp.bfloat16), value_rows, pr...  5.44 us
  transfers between devices with their start and end apart: 5, of which 5 were waited for; matrix products, arithmetic and copies ran while one was open for 7% of the time, Pallas kernels for 0%

commit v1 on v0

v1 whole, which is shorter than its diff:
```python
import jax
import jax.numpy as jnp
from jax import lax
from jax.experimental import pallas as pl
from jax.experimental.pallas import tpu as pltpu
from jax.sharding import PartitionSpec as P

HEAD_SIZE = 128
NEIGH = 5


def padded(block, sides, width):
    for axis, dim in sides:
        count = lax.axis_size(axis)
        forward = [(i, i + 1) for i in range(count - 1)]
        backward = [(target, source) for source, target in forward]
        low = lax.ppermute(
            lax.slice_in_dim(block, block.shape[dim] - width, None, axis=dim), axis, forward
        )
        high = lax.ppermute(lax.slice_in_dim(block, 0, width, axis=dim), axis, backward)
        block = jnp.concatenate([low, block, high], axis=dim)
    return block


def cross_tiles(extended):
    return jnp.stack(
        [
            extended[:, 1, 1],
            extended[:, 0, 1],
            extended[:, 2, 1],
            extended[:, 1, 0],
            extended[:, 1, 2],
        ],
        axis=1,
    )


def attend_kernel(q_ref, kv_ref, live_ref, rowok_ref, o_ref):
    kv_heads = kv_ref.shape[1] // (2 * HEAD_SIZE)
    groups = q_ref.shape[1] // (kv_heads * HEAD_SIZE)
    tok = q_ref.shape[0]
    width = kv_heads * HEAD_SIZE
    scale = HEAD_SIZE ** (-0.5)
    live = live_ref[...] > 0
    rowok = jnp.concatenate([rowok_ref[...]] * groups, axis=0) > 0
    for h in range(kv_heads):
        qh = jnp.concatenate(
            [q_ref[:, (h * groups + g) * HEAD_SIZE:(h * groups + g + 1) * HEAD_SIZE] for g in range(groups)],
            axis=0,
        )
        kh = kv_ref[:, h * HEAD_SIZE:(h + 1) * HEAD_SIZE]
        s = lax.dot_general(qh, kh, (((1,), (1,)), ((), ())), preferred_element_type=jnp.float32)
        s = s * scale
        s = jnp.where(live, s, -1e30)
        m = jnp.max(s, axis=1, keepdims=True)
        p = jnp.where(live, jnp.exp(s - m), 0.0)
        tot = jnp.sum(p, axis=1, keepdims=True)
        vh = kv_ref[:, width + h * HEAD_SIZE:width + (h + 1) * HEAD_SIZE]
        acc = jnp.dot(p.astype(jnp.bfloat16), vh, preferred_element_type=jnp.float32)
        res = jnp.where(rowok, acc / tot, 0.0).astype(o_ref.dtype)
        for g in range(groups):
            col = (h * groups + g) * HEAD_SIZE
            o_ref[:, col:col + HEAD_SIZE] = res[g * tok:(g + 1) * tok]


def attend(q, kv, live, rowok):
    tok, qw = q.shape
    keys, kw = kv.shape
    flops = 2 * 2 * tok * qw * keys
    return pl.pallas_call(
        attend_kernel,
        out_shape=jax.ShapeDtypeStruct((tok, qw), q.dtype),
        in_specs=[pl.BlockSpec(memory_space=pltpu.VMEM)] * 4,
        out_specs=pl.BlockSpec(memory_space=pltpu.VMEM),
        compiler_params=pltpu.CompilerParams(vmem_limit_bytes=48 * 1024 * 1024),
        cost_estimate=pl.CostEstimate(
            flops=flops, transcendentals=tok * qw // HEAD_SIZE * keys,
            bytes_accessed=2 * (2 * tok * qw + keys * kw)),
    )(q, kv, live, rowok)


def shards(queries, key_value, pattern, counts, span_mask):
    tok_rows = queries.shape[3]
    spans = counts.shape[0]
    my_span = lax.axis_index("span")
    my_row = lax.axis_index("ty")
    my_col = lax.axis_index("tx")
    zero_index = jnp.asarray(0).astype(jnp.int32)
    padded_counts = jnp.pad(counts, ((0, 0), (1, 1), (1, 1)))
    window = lax.dynamic_slice(padded_counts, (zero_index, my_row, my_col), (spans, 3, 3))
    near_counts = cross_tiles(window)
    own_count = lax.dynamic_index_in_dim(window[:, 1, 1], my_span, 0, keepdims=False)
    allowed = pattern.reshape(NEIGH) > 0
    span_row = lax.dynamic_index_in_dim(span_mask, my_span, 0, keepdims=False) > 0
    row_ids = jnp.arange(tok_rows, dtype=jnp.int32)
    cached = lax.all_gather(key_value, "span", axis=0, tiled=True)
    extended = padded(cached, (("ty", 1), ("tx", 2)), 1)
    kv_piece = cross_tiles(extended)
    kv_flat = kv_piece.reshape(spans * NEIGH * tok_rows, -1)
    live = (
        (row_ids[None, None, :] < near_counts[:, :, None])
        & allowed[None, :, None]
        & span_row[:, None, None]
    ).reshape(1, -1).astype(jnp.float32)
    rowok = (row_ids < own_count).astype(jnp.float32).reshape(tok_rows, 1)
    out = attend(queries.reshape(tok_rows, -1), kv_flat, live, rowok)
    return out.reshape(1, 1, 1, tok_rows, -1)


def solution(mesh):
    return jax.shard_map(
        shards,
        mesh=mesh,
        in_specs=(
            P("span", "ty", "tx", None, None),
            P("span", "ty", "tx", None, None),
            P("span", "ty", "tx", None),
            P(),
            P(),
        ),
        out_specs=P("span", "ty", "tx", None, None),
        check_vma=False,
    )
```

time: 195 us -> 168 us (0.86)
  local copies, waits for them, and re-layouts: 34.7 us -> 10.7 us
  other arithmetic: 12.6 us -> 3.4 us
  matrix products: 8.64 us -> 0 us
  Pallas kernels: 0 us -> 8.53 us
  waiting for transfers between devices: 107 us -> 115 us
    ppermute x2, waiting for transfers between devices: 51.8 us -> 78.1 us  [padded(): lax.ppermute(lax.slice_in_dim(block, block.shape[dim] - width, None, axis...]
    ppermute x2, waiting for transfers between devices: 26.3 us -> 8.18 us  [padded(): lax.ppermute(lax.slice_in_dim(block, 0, width, axis=dim), axis, backward)]
    reshape x8 -> x0, local copies, waits for them, and re-layouts: 15.1 us -> none  [the longest x4 7.99 us: shards(): key_value_block[:, :, kv_width:].reshape(-1, kv_heads, HEAD_SIZE)]
    dot_general x8 -> x0, matrix products: 8.64 us -> none  [the longest x4 5.44 us: shards(): jnp.einsum('tkgl,lkd->tkgd', weights.astype(jnp.bfloat16), value_rows, pr...]
    pallas_call x0 -> x1, Pallas kernels: none -> 8.53 us  [attend(): pl.pallas_call(attend_kernel, out_shape=jax.ShapeDtypeStruct((tok, qw), q...]
    reduce_sum x2 -> x0, other arithmetic: 5.27 us -> none  [shards(): attend_run_sum = attend_run_sum * fade_factor + jnp.sum(weights, axis=-1)]
    slice x4 -> x0, local copies, waits for them, and re-layouts: 4.96 us -> none  [shards(): key_value_block[:, :, kv_width:].reshape(-1, kv_heads, HEAD_SIZE)]
    ppermute x2, starting transfers between devices: 7.1 us -> 4.17 us  [padded(): lax.ppermute(lax.slice_in_dim(block, 0, width, axis=dim), axis, backward)]
  transfers between devices with their start and end apart: 5 -> 5, of which waited for: 5 -> 5; matrix products, arithmetic and copies ran while one was open for 7% -> 5% of each run, Pallas kernels for 0% -> 0%
where the time goes in v1:
time: 168 us; the launch traced here: 166 us
  waiting for transfers between devices  115 us (68%)
  starting transfers between devices  14.3 us (9%)
  between operations  13.5 us (8%)
  local copies, waits for them, and re-layouts  10.7 us (6%)
  Pallas kernels  8.53 us (5%)
  other arithmetic  3.4 us (2%)
    ppermute x2, waiting for transfers between devices, padded(): lax.ppermute(lax.slice_in_dim(block, block.shape[dim] - width, None, axis...  78.1 us
    all_gather x1, waiting for transfers between devices, shards(): cached = lax.all_gather(key_value, 'span', axis=0, tiled=True)  28.2 us
    ppermute x2, starting transfers between devices, padded(): lax.ppermute(lax.slice_in_dim(block, block.shape[dim] - width, None, axis...  10.1 us
    pallas_call x1, Pallas kernels, attend(): pl.pallas_call(attend_kernel, out_shape=jax.ShapeDtypeStruct((tok, qw), q...  8.53 us
    ppermute x2, waiting for transfers between devices, padded(): lax.ppermute(lax.slice_in_dim(block, 0, width, axis=dim), axis, backward)  8.18 us
    unnamed x14, local copies, waits for them, and re-layouts  5.32 us
    ppermute x2, starting transfers between devices, padded(): lax.ppermute(lax.slice_in_dim(block, 0, width, axis=dim), axis, backward)  4.17 us
  transfers between devices with their start and end apart: 5, of which 5 were waited for; matrix products, arithmetic and copies ran while one was open for 5% of the time, Pallas kernels for 0%

profile of v1, /device:TPU:95, one launch (start us, length us, event | category | flops | bytes accessed | tf_op | source)
XLA Modules:
  0.0 165.7 jit_solution(15920464151733771617)
XLA Ops:
  6.5 0.0 all-gather.2.cloned.1.call-start
  6.5 0.7 all-gather.2.cloned.1.call-update
  7.3 28.2 %all-gather.2.cloned.1.call-done = bf16[4,1,1,128,1024]{4,3,2,1,0:T(8,128)(2,1)} async-done(((bf16[1,1,1,128,1024]{4,3,2,1,0:T(8,128)(2,1)}), bf16[4,1,1,128,1024]{4,3,2,1,0:T(8,128)(2,1)}) %all-gather.2.cloned.1.call-update) | async-done | bytes 1048592 | tf_op jit(solution)/shard_map/all_gather | solution.py:96
  35.5 7.1 %collective-permute-start = (bf16[4,1,1,128,1024]{4,3,0,2,1:T(8,128)(2,1)}, bf16[4,1,1,128,1024]{4,3,0,2,1:T(8,128)(2,1)S(1)}, u32[]{:S(2)}, u32[]{:S(2)}) collective-permute-start(bf16[4,1,1,128,1024]{4,3,0,2,1:T(8,128)(2,1)} %bitcast.32), channel_id=1, source_target_pairs={{0,8},{8,16},{16,24},{24,32},{32,40},{40,48},{48,56},{1,9},{9,17},... | collective-permute-start | bytes 3145736 | tf_op jit(solution)/shard_map/ppermute | solution.py:17
  42.6 1.9 %collective-permute-start.1 = (bf16[4,1,1,128,1024]{4,3,0,2,1:T(8,128)(2,1)}, bf16[4,1,1,128,1024]{4,3,0,2,1:T(8,128)(2,1)S(1)}, u32[]{:S(2)}, u32[]{:S(2)}) collective-permute-start(bf16[4,1,1,128,1024]{4,3,0,2,1:T(8,128)(2,1)} %bitcast.33), channel_id=1, source_target_pairs={{8,0},{16,8},{24,16},{32,24},{40,32},{48,40},{56,48},{9,1},{17,9},... | collective-permute-start | bytes 3145736 | tf_op jit(solution)/shard_map/ppermute | solution.py:20
  44.5 21.3 %collective-permute-done = bf16[4,1,1,128,1024]{4,3,0,2,1:T(8,128)(2,1)S(1)} collective-permute-done((bf16[4,1,1,128,1024]{4,3,0,2,1:T(8,128)(2,1)}, bf16[4,1,1,128,1024]{4,3,0,2,1:T(8,128)(2,1)S(1)}, u32[]{:S(2)}, u32[]{:S(2)}) %collective-permute-start) | collective-permute-done | bytes 1048608 | tf_op jit(solution)/shard_map/ppermute | solution.py:17
  65.8 5.6 %collective-permute-done.1 = bf16[4,1,1,128,1024]{4,3,0,2,1:T(8,128)(2,1)S(1)} collective-permute-done((bf16[4,1,1,128,1024]{4,3,0,2,1:T(8,128)(2,1)}, bf16[4,1,1,128,1024]{4,3,0,2,1:T(8,128)(2,1)S(1)}, u32[]{:S(2)}, u32[]{:S(2)}) %collective-permute-start.1) | collective-permute-done | bytes 1048608 | tf_op jit(solution)/shard_map/ppermute | solution.py:20
  71.4 2.0 %pad_maximum_fusion = bf16[4,3,1,128,1024]{4,3,2,1,0:T(8,128)(2,1)S(1)} fusion(bf16[4,1,1,128,1024]{4,3,2,1,0:T(8,128)(2,1)S(1)} %bitcast.35, bf16[4,1,1,128,1024]{4,3,2,1,0:T(8,128)(2,1)} %all-gather.2.cloned.1.call-done, bf16[4,1,1,128,1024]{4,3,2,1,0:T(8,128)(2,1)S(1)} %bitcast.34), kind=kLoop, calls=%fused_computation | loop fusion | flops 3145728 | bytes 6291456 | tf_op jit(solution)/shard_map/concatenate | solution.py:21
  73.4 2.0 %copy.24 = bf16[4,3,1,128,1024]{4,3,0,2,1:T(8,128)(2,1)} copy(bf16[4,3,1,128,1024]{4,3,2,1,0:T(8,128)(2,1)S(1)} %pad_maximum_fusion) | data formatting | bytes 6291456 | tf_op jit(solution)/shard_map/concatenate | solution.py:21
  75.4 0.0 copy-done.1
  75.4 0.0 copy-done.2
  75.4 3.0 %collective-permute-start.2 = (bf16[4,3,1,128,1024]{4,3,0,2,1:T(8,128)(2,1)}, bf16[4,3,1,128,1024]{4,3,0,2,1:T(8,128)(2,1)}, u32[]{:S(2)}, u32[]{:S(2)}) collective-permute-start(bf16[4,3,1,128,1024]{4,3,0,2,1:T(8,128)(2,1)} %copy.24), channel_id=1, source_target_pairs={{0,1},{1,2},{2,3},{3,4},{4,5},{5,6},{6,7},{8,9},{9,10},{10,11},{11... | collective-permute-start | bytes 9437192 | tf_op jit(solution)/shard_map/ppermute | solution.py:17
  78.4 2.2 %collective-permute-start.3 = (bf16[4,3,1,128,1024]{4,3,2,1,0:T(8,128)(2,1)S(1)}, bf16[4,3,1,128,1024]{4,3,2,1,0:T(8,128)(2,1)}, u32[]{:S(2)}, u32[]{:S(2)}) collective-permute-start(bf16[4,3,1,128,1024]{4,3,2,1,0:T(8,128)(2,1)S(1)} %pad_maximum_fusion), channel_id=1, source_target_pairs={{1,0},{2,1},{3,2},{4,3},{5,4},{6,5},{7,6},{9,8},{10,9},{11,10},{12... | collective-permute-start | bytes 9437192 | tf_op jit(solution)/shard_map/ppermute | solution.py:20
  80.7 0.0 copy-done.3
  80.7 0.6 fusion.6
  81.3 0.1 copy.26
  81.4 0.6 pad_dynamic-slice_fusion
  82.0 0.7 compare_bitcast_fusion
  82.7 0.0 copy-done.4
  82.7 0.1 fusion.5
  82.8 0.7 fusion.2.rowok_ref
  83.4 1.3 bitcast_dynamic-update-slice_fusion.2
  84.7 1.3 bitcast_dynamic-update-slice_fusion.1
  86.0 1.3 bitcast_dynamic-update-slice_fusion
  87.3 56.8 %collective-permute-done.2 = bf16[4,3,1,128,1024]{4,3,0,2,1:T(8,128)(2,1)} collective-permute-done((bf16[4,3,1,128,1024]{4,3,0,2,1:T(8,128)(2,1)}, bf16[4,3,1,128,1024]{4,3,0,2,1:T(8,128)(2,1)}, u32[]{:S(2)}, u32[]{:S(2)}) %collective-permute-start.2) | collective-permute-done | bytes 3145760 | tf_op jit(solution)/shard_map/ppermute | solution.py:17
  144.1 1.3 fusion.1
  145.4 2.6 %collective-permute-done.3 = bf16[4,3,1,128,1024]{4,3,2,1,0:T(8,128)(2,1)} collective-permute-done((bf16[4,3,1,128,1024]{4,3,2,1,0:T(8,128)(2,1)S(1)}, bf16[4,3,1,128,1024]{4,3,2,1,0:T(8,128)(2,1)}, u32[]{:S(2)}, u32[]{:S(2)}) %collective-permute-start.3) | collective-permute-done | bytes 3145760 | tf_op jit(solution)/shard_map/ppermute | solution.py:20
  148.0 1.3 fusion
  149.3 0.0 copy-start
  149.3 0.9 copy.25
  150.2 0.1 copy-done
  150.3 8.5 %shard_map.55 = bf16[128,1536]{1,0:T(8,128)(2,1)} custom-call(bf16[128,1536]{1,0:T(8,128)(2,1)S(1)} %bitcast.31, bf16[2560,1024]{1,0:T(8,128)(2,1)S(1)} %bitcast.30, f32[1,2560]{1,0:T(1,128)S(1)} %reshape.93.live_ref, f32[128,1]{1,0:T(8,128)S(1)} %fusion.2.rowok_ref), custom_call_target="tpu_custom_call" | custom-call | flops 2013265920 | bytes 6029312 | tf_op jit(solution)/shard_map/pallas_call | solution.py:70
  (7 shorter events, 0.1 us)
Async XLA Ops:
  6.5 29.0 %all-gather.2.cloned.1.call-start = ((), (), s32[]{:S(2)}) async-start(), calls=%async_computation | async-start | bytes 1310720 | tf_op jit(solution)/shard_map/all_gather | solution.py:96
  35.5 30.3 %collective-permute-start = (bf16[4,1,1,128,1024]{4,3,0,2,1:T(8,128)(2,1)}, bf16[4,1,1,128,1024]{4,3,0,2,1:T(8,128)(2,1)S(1)}, u32[]{:S(2)}, u32[]{:S(2)}) collective-permute-start(bf16[4,1,1,128,1024]{4,3,0,2,1:T(8,128)(2,1)} %bitcast.32), channel_id=1, source_target_pairs={{0,8},{8,16},{16,24},{24,32},{32,40},{40,48},{48,56},{1,9},{9,17},... | collective-permute-start | bytes 3145736 | tf_op jit(solution)/shard_map/ppermute | solution.py:17
  42.6 28.8 %collective-permute-start.1 = (bf16[4,1,1,128,1024]{4,3,0,2,1:T(8,128)(2,1)}, bf16[4,1,1,128,1024]{4,3,0,2,1:T(8,128)(2,1)S(1)}, u32[]{:S(2)}, u32[]{:S(2)}) collective-permute-start(bf16[4,1,1,128,1024]{4,3,0,2,1:T(8,128)(2,1)} %bitcast.33), channel_id=1, source_target_pairs={{8,0},{16,8},{24,16},{32,24},{40,32},{48,40},{56,48},{9,1},{17,9},... | collective-permute-start | bytes 3145736 | tf_op jit(solution)/shard_map/ppermute | solution.py:20
  65.8 9.5 %copy-start.1 = (bf16[4,1,1,128,1024]{4,3,0,2,1:T(8,128)(2,1)}, bf16[4,1,1,128,1024]{4,3,0,2,1:T(8,128)(2,1)S(1)}, u32[]{:S(2)}) copy-start(bf16[4,1,1,128,1024]{4,3,0,2,1:T(8,128)(2,1)S(1)} %collective-permute-done) | copy-start | bytes 3145732
  71.4 4.0 %copy-start.2 = (bf16[4,1,1,128,1024]{4,3,0,2,1:T(8,128)(2,1)}, bf16[4,1,1,128,1024]{4,3,0,2,1:T(8,128)(2,1)S(1)}, u32[]{:S(2)}) copy-start(bf16[4,1,1,128,1024]{4,3,0,2,1:T(8,128)(2,1)S(1)} %collective-permute-done.1) | copy-start | bytes 3145732
  71.4 9.3 %copy-start.3 = (s32[4,8,8]{2,1,0:T(8,128)S(1)}, s32[4,8,8]{2,1,0:T(8,128)}, u32[]{:S(2)}) copy-start(s32[4,8,8]{2,1,0:T(8,128)} %param.8) | copy-start | bytes 3076
  71.4 11.2 %copy-start.4 = (s32[1,1,1,5]{3,2,1,0:T(1,128)S(1)}, s32[1,1,1,5]{3,2,1,0:T(1,128)}, u32[]{:S(2)}) copy-start(s32[1,1,1,5]{3,2,1,0:T(1,128)} %param.7) | copy-start | bytes 64
  75.4 68.7 %collective-permute-start.2 = (bf16[4,3,1,128,1024]{4,3,0,2,1:T(8,128)(2,1)}, bf16[4,3,1,128,1024]{4,3,0,2,1:T(8,128)(2,1)}, u32[]{:S(2)}, u32[]{:S(2)}) collective-permute-start(bf16[4,3,1,128,1024]{4,3,0,2,1:T(8,128)(2,1)} %copy.24), channel_id=1, source_target_pairs={{0,1},{1,2},{2,3},{3,4},{4,5},{5,6},{6,7},{8,9},{9,10},{10,11},{11... | collective-permute-start | bytes 9437192 | tf_op jit(solution)/shard_map/ppermute | solution.py:17
  78.4 69.6 %collective-permute-start.3 = (bf16[4,3,1,128,1024]{4,3,2,1,0:T(8,128)(2,1)S(1)}, bf16[4,3,1,128,1024]{4,3,2,1,0:T(8,128)(2,1)}, u32[]{:S(2)}, u32[]{:S(2)}) collective-permute-start(bf16[4,3,1,128,1024]{4,3,2,1,0:T(8,128)(2,1)S(1)} %pad_maximum_fusion), channel_id=1, source_target_pairs={{1,0},{2,1},{3,2},{4,3},{5,4},{6,5},{7,6},{9,8},{10,9},{11,10},{12... | collective-permute-start | bytes 9437192 | tf_op jit(solution)/shard_map/ppermute | solution.py:20
  149.3 1.0 copy-start
Sparse Core Ops, SparseCore 0:
  9.2 26.2 all-gather.1

commit v2 on v1

--- a/solution.py
+++ b/solution.py
@@ -7,19 +7,8 @@
 
 HEAD_SIZE = 128
 NEIGH = 5
-
-
-def padded(block, sides, width):
-    for axis, dim in sides:
-        count = lax.axis_size(axis)
-        forward = [(i, i + 1) for i in range(count - 1)]
-        backward = [(target, source) for source, target in forward]
-        low = lax.ppermute(
-            lax.slice_in_dim(block, block.shape[dim] - width, None, axis=dim), axis, forward
-        )
-        high = lax.ppermute(lax.slice_in_dim(block, 0, width, axis=dim), axis, backward)
-        block = jnp.concatenate([low, block, high], axis=dim)
-    return block
+OFFSETS = ((0, 0), (-1, 0), (1, 0), (0, -1), (0, 1))
+INVERSE = (0, 2, 1, 4, 3)
 
 
 def cross_tiles(extended):
@@ -35,7 +24,7 @@
     )
 
 
-def attend_kernel(q_ref, kv_ref, live_ref, rowok_ref, o_ref):
+def attend_body(q_ref, kv_ref, live_ref, rowok_ref, o_ref):
     kv_heads = kv_ref.shape[1] // (2 * HEAD_SIZE)
     groups = q_ref.shape[1] // (kv_heads * HEAD_SIZE)
     tok = q_ref.shape[0]
@@ -63,16 +52,137 @@
             o_ref[:, col:col + HEAD_SIZE] = res[g * tok:(g + 1) * tok]
 
 
-def attend(q, kv, live, rowok):
+def window_kernel(spans, rows, cols, q_ref, kv_ref, live_ref, rowok_ref, o_ref,
+                  kvbuf, send_sem, recv_sem, local_sem):
+    tok = kv_ref.shape[0]
+    c = lax.axis_index("span")
+    i = lax.axis_index("ty")
+    j = lax.axis_index("tx")
+
+    def inside(d):
+        dy, dx = OFFSETS[d]
+        y, x = i + dy, j + dx
+        return (y >= 0) & (y < rows) & (x >= 0) & (x < cols)
+
+    def slot(s, o):
+        return kvbuf.at[pl.ds((s * NEIGH + o) * tok, tok), :]
+
+    n_nb = sum(inside(d).astype(jnp.int32) for d in range(1, NEIGH))
+
+    barrier = pltpu.get_barrier_semaphore()
+    for s in range(spans):
+        @pl.when(s != c)
+        def _():
+            pl.semaphore_signal(barrier, 1, device_id=(s, i, j), device_id_type=pl.DeviceIdType.MESH)
+    for d in range(1, NEIGH):
+        dy, dx = OFFSETS[d]
+        @pl.when(inside(d))
+        def _():
+            pl.semaphore_signal(barrier, 1, device_id=(c, i + dy, j + dx), device_id_type=pl.DeviceIdType.MESH)
+    pl.semaphore_wait(barrier, spans - 1 + n_nb)
+
+    def up_copy(s):
+        return pltpu.make_async_remote_copy(
+            src_ref=kv_ref, dst_ref=slot(c, 0), send_sem=send_sem.at[s], recv_sem=recv_sem.at[c * NEIGH],
+            device_id=(s, i, j), device_id_type=pl.DeviceIdType.MESH)
+
+    def side_copy(s, d, src):
+        dy, dx = OFFSETS[d]
+        return pltpu.make_async_remote_copy(
+            src_ref=src, dst_ref=slot(s, INVERSE[d]),
+            send_sem=send_sem.at[spans + s * (NEIGH - 1) + d - 1],
+            recv_sem=recv_sem.at[s * NEIGH + INVERSE[d]],
+            device_id=(c, i + dy, j + dx), device_id_type=pl.DeviceIdType.MESH)
+
+    for s in range(spans):
+        @pl.when(s > c)
+        def _():
+            up_copy(s).start()
+
+    for s in range(spans):
+        @pl.when(s == c)
+        def _():
+            for d in range(1, NEIGH):
+                @pl.when(inside(d))
+                def _():
+                    side_copy(s, d, kv_ref).start()
+
+    own = pltpu.make_async_copy(kv_ref, slot(0, 0), local_sem.at[0])
+    for s in range(spans):
+        @pl.when(s == c)
+        def _():
+            pltpu.make_async_copy(kv_ref, slot(s, 0), local_sem.at[0]).start()
+
+    zeros = jnp.zeros((tok, kv_ref.shape[1]), kv_ref.dtype)
+    for s in range(spans):
+        @pl.when(s > c)
+        def _():
+            for o in range(NEIGH):
+                slot(s, o)[...] = zeros
+        @pl.when(s <= c)
+        def _():
+            for d in range(1, NEIGH):
+                @pl.when(jnp.logical_not(inside(INVERSE[d])))
+                def _():
+                    slot(s, INVERSE[d])[...] = zeros
+
+    for s in range(spans):
+        @pl.when(s < c)
+        def _():
+            pltpu.make_async_remote_copy(
+                src_ref=kv_ref, dst_ref=slot(s, 0), send_sem=send_sem.at[s], recv_sem=recv_sem.at[s * NEIGH],
+                device_id=(s, i, j), device_id_type=pl.DeviceIdType.MESH).wait_recv()
+            for d in range(1, NEIGH):
+                @pl.when(inside(d))
+                def _():
+                    side_copy(s, d, slot(s, 0)).start()
+
+    for s in range(spans):
+        @pl.when(s <= c)
+        def _():
+            for o in range(1, NEIGH):
+                dy, dx = OFFSETS[o]
+                @pl.when(inside(o))
+                def _():
+                    pltpu.make_async_remote_copy(
+                        src_ref=kv_ref, dst_ref=slot(s, o), send_sem=send_sem.at[0],
+                        recv_sem=recv_sem.at[s * NEIGH + o],
+                        device_id=(c, i + dy, j + dx), device_id_type=pl.DeviceIdType.MESH).wait_recv()
+
+    for s in range(spans):
+        @pl.when(s > c)
+        def _():
+            up_copy(s).wait_send()
+        @pl.when(s <= c)
+        def _():
+            for d in range(1, NEIGH):
+                @pl.when(inside(d))
+                def _():
+                    side_copy(s, d, kv_ref).wait_send()
+    own.wait()
+
+    attend_body(q_ref, kvbuf, live_ref, rowok_ref, o_ref)
+
+
+def window_attend(q, kv, live, rowok, spans, rows, cols):
     tok, qw = q.shape
-    keys, kw = kv.shape
+    kw = kv.shape[1]
+    keys = spans * NEIGH * tok
     flops = 2 * 2 * tok * qw * keys
+    kernel = lambda *refs: window_kernel(spans, rows, cols, *refs)
     return pl.pallas_call(
-        attend_kernel,
+        kernel,
         out_shape=jax.ShapeDtypeStruct((tok, qw), q.dtype),
         in_specs=[pl.BlockSpec(memory_space=pltpu.VMEM)] * 4,
         out_specs=pl.BlockSpec(memory_space=pltpu.VMEM),
-        compiler_params=pltpu.CompilerParams(vmem_limit_bytes=48 * 1024 * 1024),
+        scratch_shapes=[
+            pltpu.VMEM((keys, kw), kv.dtype),
+            pltpu.SemaphoreType.DMA((spans + spans * (NEIGH - 1),)),
+            pltpu.SemaphoreType.DMA((spans * NEIGH,)),
+            pltpu.SemaphoreType.DMA((1,)),
+        ],
+        compiler_params=pltpu.CompilerParams(
+            vmem_limit_bytes=48 * 1024 * 1024, collective_id=0, has_side_effects=True),
         cost_estimate=pl.CostEstimate(
             flops=flops, transcendentals=tok * qw // HEAD_SIZE * keys,
             bytes_accessed=2 * (2 * tok * qw + keys * kw)),
@@ -81,7 +191,7 @@
 
 def shards(queries, key_value, pattern, counts, span_mask):
     tok_rows = queries.shape[3]
-    spans = counts.shape[0]
+    spans, rows, cols = counts.shape
     my_span = lax.axis_index("span")
     my_row = lax.axis_index("ty")
     my_col = lax.axis_index("tx")
@@ -93,17 +203,14 @@
     allowed = pattern.reshape(NEIGH) > 0
     span_row = lax.dynamic_index_in_dim(span_mask, my_span, 0, keepdims=False) > 0
     row_ids = jnp.arange(tok_rows, dtype=jnp.int32)
-    cached = lax.all_gather(key_value, "span", axis=0, tiled=True)
-    extended = padded(cached, (("ty", 1), ("tx", 2)), 1)
-    kv_piece = cross_tiles(extended)
-    kv_flat = kv_piece.reshape(spans * NEIGH * tok_rows, -1)
     live = (
         (row_ids[None, None, :] < near_counts[:, :, None])
         & allowed[None, :, None]
         & span_row[:, None, None]
     ).reshape(1, -1).astype(jnp.float32)
     rowok = (row_ids < own_count).astype(jnp.float32).reshape(tok_rows, 1)
-    out = attend(queries.reshape(tok_rows, -1), kv_flat, live, rowok)
+    out = window_attend(
+        queries.reshape(tok_rows, -1), key_value.reshape(tok_rows, -1), live, rowok, spans, rows, cols)
     return out.reshape(1, 1, 1, tok_rows, -1)
 
 

time: 168 us -> 68 us (0.40)
  the two profiles are of different devices: /device:TPU:95 before, /device:TPU:121 now
where the time goes in v2:
time: 68 us; the launch traced here: 67.7 us
  Pallas kernels  60.9 us (90%)
  local copies, waits for them, and re-layouts  5.34 us (8%)
  other arithmetic  1.43 us (2%)
    pallas_call x1, Pallas kernels, window_attend(): pl.pallas_call(kernel, out_shape=jax.ShapeDtypeStruct((tok, qw), q.dtype)...  60.9 us
    unnamed x9, local copies, waits for them, and re-layouts  4.06 us

profile of v2, /device:TPU:121, one launch (start us, length us, event | category | flops | bytes accessed | tf_op | source)
XLA Modules:
  0.0 67.7 jit_solution(12096311663700632848)
XLA Ops:
  0.0 0.0 copy-start.2
  0.0 0.7 %copy-done.2 = s32[4,8,8]{2,1,0:T(8,128)S(1)} copy-done((s32[4,8,8]{2,1,0:T(8,128)S(1)}, s32[4,8,8]{2,1,0:T(8,128)}, u32[]{:S(2)}) %copy-start.2) | copy-done | bytes 1048
  0.7 0.6 pad_dynamic-slice_fusion
  1.3 0.6 fusion.4
  1.9 0.7 %compare_bitcast_fusion = pred[4]{0:T(512)(128)(4,1)S(1)} fusion(s32[4,4]{1,0:T(4,128)} %param.9, s32[]{:T(128)S(6)} %select_n.14), kind=kLoop, calls=%fused_computation.17 | loop fusion | flops 4 | bytes 24 | tf_op jit(solution)/shard_map/gt | solution.py:204
  2.6 0.0 copy-start.3
  2.6 0.7 copy-done.3
  3.2 0.1 copy.7
  3.3 0.1 fusion.3
  3.4 0.7 fusion.refs_3_
  4.1 0.0 copy-start
  4.1 1.0 %copy-done = bf16[1,1,1,128,1536]{4,3,2,1,0:T(8,128)(2,1)S(1)} copy-done((bf16[1,1,1,128,1536]{4,3,2,1,0:T(8,128)(2,1)S(1)}, bf16[1,1,1,128,1536]{4,3,2,1,0:T(8,128)(2,1)}, u32[]{:S(2)}) %copy-start) | copy-done | bytes 393240
  5.1 0.0 copy-start.1
  5.1 0.9 %copy-done.1 = bf16[1,1,1,128,1024]{4,3,2,1,0:T(8,128)(2,1)S(1)} copy-done((bf16[1,1,1,128,1024]{4,3,2,1,0:T(8,128)(2,1)S(1)}, bf16[1,1,1,128,1024]{4,3,2,1,0:T(8,128)(2,1)}, u32[]{:S(2)}) %copy-start.1) | copy-done | bytes 262168
  6.1 60.9 %shard_map.55 = bf16[128,1536]{1,0:T(8,128)(2,1)S(1)} custom-call(bf16[128,1536]{1,0:T(8,128)(2,1)S(1)} %bitcast.14, bf16[128,1024]{1,0:T(8,128)(2,1)S(1)} %bitcast.15, f32[1,2560]{1,0:T(1,128)S(1)} %reshape.93.refs_2_, f32[128,1]{1,0:T(8,128)S(1)} %fusion.refs_3_), custom_call_target="tpu_custom_call" | custom-call | flops 2013265920 | bytes 6029312 | tf_op jit(solution)/shard_map/pallas_call | solution.py:173
  67.0 0.7 %copy.9 = bf16[1,1,1,128,1536]{4,3,2,1,0:T(8,128)(2,1)} copy(bf16[1,1,1,128,1536]{4,3,2,1,0:T(8,128)(2,1)S(1)} %bitcast.13) | data formatting | bytes 786432
  (3 shorter events, 0.0 us)
Async XLA Ops:
  0.0 0.7 %copy-start.2 = (s32[4,8,8]{2,1,0:T(8,128)S(1)}, s32[4,8,8]{2,1,0:T(8,128)}, u32[]{:S(2)}) copy-start(s32[4,8,8]{2,1,0:T(8,128)} %param.8) | copy-start | bytes 3076
  2.6 0.7 copy-start.3
  4.1 1.0 %copy-start = (bf16[1,1,1,128,1536]{4,3,2,1,0:T(8,128)(2,1)S(1)}, bf16[1,1,1,128,1536]{4,3,2,1,0:T(8,128)(2,1)}, u32[]{:S(2)}) copy-start(bf16[1,1,1,128,1536]{4,3,2,1,0:T(8,128)(2,1)} %param.5) | copy-start | bytes 1179652
  5.1 0.9 %copy-start.1 = (bf16[1,1,1,128,1024]{4,3,2,1,0:T(8,128)(2,1)S(1)}, bf16[1,1,1,128,1024]{4,3,2,1,0:T(8,128)(2,1)}, u32[]{:S(2)}) copy-start(bf16[1,1,1,128,1024]{4,3,2,1,0:T(8,128)(2,1)} %param.6) | copy-start | bytes 786436

commit v3 on v2

--- a/solution.py
+++ b/solution.py
@@ -53,11 +53,19 @@
 
 
 def window_kernel(spans, rows, cols, q_ref, kv_ref, live_ref, rowok_ref, o_ref,
-                  kvbuf, send_sem, recv_sem, local_sem):
+                  kvbuf, trans, send_sem, recv_sem, fwd_sem, trans_sem, local_sem):
     tok = kv_ref.shape[0]
     c = lax.axis_index("span")
     i = lax.axis_index("ty")
     j = lax.axis_index("tx")
+    mesh_id = pl.DeviceIdType.MESH
+    relayed = cols >= 4
+    half = cols // 2
+    is_a = j == half - 1
+    is_b = j == half
+
+    def relay_col(s):
+        return 0 if s % 2 == 0 else cols - 1
 
     def inside(d):
         dy, dx = OFFSETS[d]
@@ -67,24 +75,42 @@
     def slot(s, o):
         return kvbuf.at[pl.ds((s * NEIGH + o) * tok, tok), :]
 
+    def boundary(d):
+        if not relayed or d not in (3, 4):
+            return None
+        return is_a if d == 4 else is_b
+
     n_nb = sum(inside(d).astype(jnp.int32) for d in range(1, NEIGH))
+    ends = (is_a | is_b | (j == 0) | (j == cols - 1)) if relayed else (j < 0)
+    n_extra = jnp.where(ends, 2, 0)
 
     barrier = pltpu.get_barrier_semaphore()
+    def greet(target):
+        pl.semaphore_signal(barrier, 1, device_id=target, device_id_type=mesh_id)
     for s in range(spans):
         @pl.when(s != c)
         def _():
-            pl.semaphore_signal(barrier, 1, device_id=(s, i, j), device_id_type=pl.DeviceIdType.MESH)
+            greet((s, i, j))
     for d in range(1, NEIGH):
         dy, dx = OFFSETS[d]
         @pl.when(inside(d))
         def _():
-            pl.semaphore_signal(barrier, 1, device_id=(c, i + dy, j + dx), device_id_type=pl.DeviceIdType.MESH)
-    pl.semaphore_wait(barrier, spans - 1 + n_nb)
+            greet((c, i + dy, j + dx))
+    if relayed:
+        @pl.when(is_a | is_b)
+        def _():
+            greet((c, i, 0))
+            greet((c, i, cols - 1))
+        @pl.when((j == 0) | (j == cols - 1))
+        def _():
+            greet((c, i, half - 1))
+            greet((c, i, half))
+    pl.semaphore_wait(barrier, spans - 1 + n_nb + n_extra)
 
     def up_copy(s):
         return pltpu.make_async_remote_copy(
             src_ref=kv_ref, dst_ref=slot(c, 0), send_sem=send_sem.at[s], recv_sem=recv_sem.at[c * NEIGH],
-            device_id=(s, i, j), device_id_type=pl.DeviceIdType.MESH)
+            device_id=(s, i, j), device_id_type=mesh_id)
 
     def side_copy(s, d, src):
         dy, dx = OFFSETS[d]
@@ -92,7 +118,48 @@
             src_ref=src, dst_ref=slot(s, INVERSE[d]),
             send_sem=send_sem.at[spans + s * (NEIGH - 1) + d - 1],
             recv_sem=recv_sem.at[s * NEIGH + INVERSE[d]],
-            device_id=(c, i + dy, j + dx), device_id_type=pl.DeviceIdType.MESH)
+            device_id=(c, i + dy, j + dx), device_id_type=mesh_id)
+
+    def to_relay(s, d, src):
+        way = 0 if d == 4 else 1
+        return pltpu.make_async_remote_copy(
+            src_ref=src, dst_ref=trans.at[way, s],
+            send_sem=send_sem.at[spans + s * (NEIGH - 1) + d - 1],
+            recv_sem=trans_sem.at[way, s],
+            device_id=(c, i, relay_col(s)), device_id_type=mesh_id)
+
+    def from_relay(s, way):
+        target = half if way == 0 else half - 1
+        o = 3 if way == 0 else 4
+        return pltpu.make_async_remote_copy(
+            src_ref=trans.at[way, s], dst_ref=slot(s, o),
+            send_sem=fwd_sem.at[way, s], recv_sem=recv_sem.at[s * NEIGH + o],
+            device_id=(c, i, target), device_id_type=mesh_id)
+
+    def send_side(s, d, src, wait=False):
+        bnd = boundary(d)
+        direct = inside(d) if bnd is None else inside(d) & jnp.logical_not(bnd)
+        @pl.when(direct)
+        def _():
+            cp = side_copy(s, d, src)
+            cp.wait_send() if wait else cp.start()
+        if bnd is not None:
+            @pl.when(bnd)
+            def _():
+                cp = to_relay(s, d, src)
+                cp.wait_send() if wait else cp.start()
+
+    def relay(s, wait=False):
+        if not relayed:
+            return
+        @pl.when(j == relay_col(s))
+        def _():
+            for way in (0, 1):
+                if wait:
+                    from_relay(s, way).wait_send()
+                else:
+                    to_relay(s, 4 if way == 0 else 3, kv_ref).wait_recv()
+                    from_relay(s, way).start()
 
     for s in range(spans):
         @pl.when(s > c)
@@ -103,9 +170,7 @@
         @pl.when(s == c)
         def _():
             for d in range(1, NEIGH):
-                @pl.when(inside(d))
-                def _():
-                    side_copy(s, d, kv_ref).start()
+                send_side(s, d, kv_ref)
 
     own = pltpu.make_async_copy(kv_ref, slot(0, 0), local_sem.at[0])
     for s in range(spans):
@@ -127,15 +192,19 @@
                     slot(s, INVERSE[d])[...] = zeros
 
     for s in range(spans):
+        @pl.when(s == c)
+        def _():
+            relay(s)
+
+    for s in range(spans):
         @pl.when(s < c)
         def _():
             pltpu.make_async_remote_copy(
                 src_ref=kv_ref, dst_ref=slot(s, 0), send_sem=send_sem.at[s], recv_sem=recv_sem.at[s * NEIGH],
-                device_id=(s, i, j), device_id_type=pl.DeviceIdType.MESH).wait_recv()
+                device_id=(s, i, j), device_id_type=mesh_id).wait_recv()
             for d in range(1, NEIGH):
-                @pl.when(inside(d))
-                def _():
-                    side_copy(s, d, slot(s, 0)).start()
+                send_side(s, d, slot(s, 0))
+            relay(s)
 
     for s in range(spans):
         @pl.when(s <= c)
@@ -147,7 +216,7 @@
                     pltpu.make_async_remote_copy(
                         src_ref=kv_ref, dst_ref=slot(s, o), send_sem=send_sem.at[0],
                         recv_sem=recv_sem.at[s * NEIGH + o],
-                        device_id=(c, i + dy, j + dx), device_id_type=pl.DeviceIdType.MESH).wait_recv()
+                        device_id=(c, i + dy, j + dx), device_id_type=mesh_id).wait_recv()
 
     for s in range(spans):
         @pl.when(s > c)
@@ -156,9 +225,8 @@
         @pl.when(s <= c)
         def _():
             for d in range(1, NEIGH):
-                @pl.when(inside(d))
-                def _():
-                    side_copy(s, d, kv_ref).wait_send()
+                send_side(s, d, kv_ref, wait=True)
+            relay(s, wait=True)
     own.wait()
 
     attend_body(q_ref, kvbuf, live_ref, rowok_ref, o_ref)
@@ -177,8 +245,11 @@
         out_specs=pl.BlockSpec(memory_space=pltpu.VMEM),
         scratch_shapes=[
             pltpu.VMEM((keys, kw), kv.dtype),
+            pltpu.VMEM((2, spans, tok, kw), kv.dtype),
             pltpu.SemaphoreType.DMA((spans + spans * (NEIGH - 1),)),
             pltpu.SemaphoreType.DMA((spans * NEIGH,)),
+            pltpu.SemaphoreType.DMA((2, spans)),
+            pltpu.SemaphoreType.DMA((2, spans)),
             pltpu.SemaphoreType.DMA((1,)),
         ],
         compiler_params=pltpu.CompilerParams(

time: 68 us -> 67 us (0.985)
  the two profiles are of different devices: /device:TPU:121 before, /device:TPU:94 now
where the time goes in v3:
time: 67 us; the launch traced here: 66.8 us
  Pallas kernels  60 us (90%)
  local copies, waits for them, and re-layouts  5.34 us (8%)
  other arithmetic  1.43 us (2%)
    pallas_call x1, Pallas kernels, window_attend(): pl.pallas_call(kernel, out_shape=jax.ShapeDtypeStruct((tok, qw), q.dtype)...  60 us
    unnamed x9, local copies, waits for them, and re-layouts  4.06 us

profile of v3, /device:TPU:94, one launch (start us, length us, event | category | flops | bytes accessed | tf_op | source)
XLA Modules:
  0.0 66.8 jit_solution(7652537858544961304)
XLA Ops:
  0.0 0.0 copy-start.2
  0.0 0.7 %copy-done.2 = s32[4,8,8]{2,1,0:T(8,128)S(1)} copy-done((s32[4,8,8]{2,1,0:T(8,128)S(1)}, s32[4,8,8]{2,1,0:T(8,128)}, u32[]{:S(2)}) %copy-start.2) | copy-done | bytes 1048
  0.7 0.6 pad_dynamic-slice_fusion
  1.3 0.6 fusion.4
  1.9 0.7 %compare_bitcast_fusion = pred[4]{0:T(512)(128)(4,1)S(1)} fusion(s32[4,4]{1,0:T(4,128)} %param.9, s32[]{:T(128)S(6)} %select_n.14), kind=kLoop, calls=%fused_computation.17 | loop fusion | flops 4 | bytes 24 | tf_op jit(solution)/shard_map/gt | solution.py:275
  2.6 0.0 copy-start.3
  2.6 0.7 copy-done.3
  3.2 0.1 copy.7
  3.3 0.1 fusion.3
  3.4 0.7 fusion.refs_3_
  4.1 0.0 copy-start
  4.1 1.0 %copy-done = bf16[1,1,1,128,1536]{4,3,2,1,0:T(8,128)(2,1)S(1)} copy-done((bf16[1,1,1,128,1536]{4,3,2,1,0:T(8,128)(2,1)S(1)}, bf16[1,1,1,128,1536]{4,3,2,1,0:T(8,128)(2,1)}, u32[]{:S(2)}) %copy-start) | copy-done | bytes 393240
  5.1 0.0 copy-start.1
  5.1 0.9 %copy-done.1 = bf16[1,1,1,128,1024]{4,3,2,1,0:T(8,128)(2,1)S(1)} copy-done((bf16[1,1,1,128,1024]{4,3,2,1,0:T(8,128)(2,1)S(1)}, bf16[1,1,1,128,1024]{4,3,2,1,0:T(8,128)(2,1)}, u32[]{:S(2)}) %copy-start.1) | copy-done | bytes 262168
  6.1 60.0 %shard_map.55 = bf16[128,1536]{1,0:T(8,128)(2,1)S(1)} custom-call(bf16[128,1536]{1,0:T(8,128)(2,1)S(1)} %bitcast.14, bf16[128,1024]{1,0:T(8,128)(2,1)S(1)} %bitcast.15, f32[1,2560]{1,0:T(1,128)S(1)} %reshape.93.refs_2_, f32[128,1]{1,0:T(8,128)S(1)} %fusion.refs_3_), custom_call_target="tpu_custom_call" | custom-call | flops 2013265920 | bytes 6029312 | tf_op jit(solution)/shard_map/pallas_call | solution.py:241
  66.0 0.7 %copy.9 = bf16[1,1,1,128,1536]{4,3,2,1,0:T(8,128)(2,1)} copy(bf16[1,1,1,128,1536]{4,3,2,1,0:T(8,128)(2,1)S(1)} %bitcast.13) | data formatting | bytes 786432
  (3 shorter events, 0.0 us)
Async XLA Ops:
  0.0 0.7 %copy-start.2 = (s32[4,8,8]{2,1,0:T(8,128)S(1)}, s32[4,8,8]{2,1,0:T(8,128)}, u32[]{:S(2)}) copy-start(s32[4,8,8]{2,1,0:T(8,128)} %param.8) | copy-start | bytes 3076
  2.6 0.7 copy-start.3
  4.1 1.0 %copy-start = (bf16[1,1,1,128,1536]{4,3,2,1,0:T(8,128)(2,1)S(1)}, bf16[1,1,1,128,1536]{4,3,2,1,0:T(8,128)(2,1)}, u32[]{:S(2)}) copy-start(bf16[1,1,1,128,1536]{4,3,2,1,0:T(8,128)(2,1)} %param.5) | copy-start | bytes 1179652
  5.1 0.9 %copy-start.1 = (bf16[1,1,1,128,1024]{4,3,2,1,0:T(8,128)(2,1)S(1)}, bf16[1,1,1,128,1024]{4,3,2,1,0:T(8,128)(2,1)}, u32[]{:S(2)}) copy-start(bf16[1,1,1,128,1024]{4,3,2,1,0:T(8,128)(2,1)} %param.6) | copy-start | bytes 786436

commit v4 on v3

--- a/solution.py
+++ b/solution.py
@@ -52,8 +52,8 @@
             o_ref[:, col:col + HEAD_SIZE] = res[g * tok:(g + 1) * tok]
 
 
-def window_kernel(spans, rows, cols, q_ref, kv_ref, live_ref, rowok_ref, o_ref,
-                  kvbuf, trans, send_sem, recv_sem, fwd_sem, trans_sem, local_sem):
+def window_kernel(spans, rows, cols, q_hbm, kv_ref, live_ref, rowok_ref, o_ref,
+                  q_ref, kvbuf, trans, send_sem, recv_sem, fwd_sem, trans_sem, local_sem):
     tok = kv_ref.shape[0]
     c = lax.axis_index("span")
     i = lax.axis_index("ty")
@@ -161,6 +161,9 @@
                     to_relay(s, 4 if way == 0 else 3, kv_ref).wait_recv()
                     from_relay(s, way).start()
 
+    q_load = pltpu.make_async_copy(q_hbm, q_ref, local_sem.at[1])
+    q_load.start()
+
     for s in range(spans):
         @pl.when(s > c)
         def _():
@@ -196,15 +199,19 @@
         def _():
             relay(s)
 
-    for s in range(spans):
-        @pl.when(s < c)
-        def _():
-            pltpu.make_async_remote_copy(
-                src_ref=kv_ref, dst_ref=slot(s, 0), send_sem=send_sem.at[s], recv_sem=recv_sem.at[s * NEIGH],
-                device_id=(s, i, j), device_id_type=mesh_id).wait_recv()
-            for d in range(1, NEIGH):
-                send_side(s, d, slot(s, 0))
-            relay(s)
+    def ring_gap(a, b):
+        return min((a - b) % spans, (b - a) % spans)
+
+    for cc in range(spans):
+        @pl.when(c == cc)
+        def _():
+            for s in sorted(range(cc), key=lambda s: (ring_gap(s, cc), -s)):
+                pltpu.make_async_remote_copy(
+                    src_ref=kv_ref, dst_ref=slot(s, 0), send_sem=send_sem.at[s], recv_sem=recv_sem.at[s * NEIGH],
+                    device_id=(s, i, j), device_id_type=mesh_id).wait_recv()
+                for d in range(1, NEIGH):
+                    send_side(s, d, slot(s, 0))
+                relay(s)
 
     for s in range(spans):
         @pl.when(s <= c)
@@ -228,6 +235,7 @@
                 send_side(s, d, kv_ref, wait=True)
             relay(s, wait=True)
     own.wait()
+    q_load.wait()
 
     attend_body(q_ref, kvbuf, live_ref, rowok_ref, o_ref)
 
@@ -241,19 +249,20 @@
     return pl.pallas_call(
         kernel,
         out_shape=jax.ShapeDtypeStruct((tok, qw), q.dtype),
-        in_specs=[pl.BlockSpec(memory_space=pltpu.VMEM)] * 4,
+        in_specs=[pl.BlockSpec(memory_space=pl.ANY)] * 2 + [pl.BlockSpec(memory_space=pltpu.VMEM)] * 2,
         out_specs=pl.BlockSpec(memory_space=pltpu.VMEM),
         scratch_shapes=[
+            pltpu.VMEM((tok, qw), q.dtype),
             pltpu.VMEM((keys, kw), kv.dtype),
             pltpu.VMEM((2, spans, tok, kw), kv.dtype),
             pltpu.SemaphoreType.DMA((spans + spans * (NEIGH - 1),)),
             pltpu.SemaphoreType.DMA((spans * NEIGH,)),
             pltpu.SemaphoreType.DMA((2, spans)),
             pltpu.SemaphoreType.DMA((2, spans)),
-            pltpu.SemaphoreType.DMA((1,)),
+            pltpu.SemaphoreType.DMA((2,)),
         ],
         compiler_params=pltpu.CompilerParams(
-            vmem_limit_bytes=48 * 1024 * 1024, collective_id=0, has_side_effects=True),
+            vmem_limit_bytes=67043328, collective_id=0, has_side_effects=True),
         cost_estimate=pl.CostEstimate(
             flops=flops, transcendentals=tok * qw // HEAD_SIZE * keys,
             bytes_accessed=2 * (2 * tok * qw + keys * kw)),

time: 67 us -> 63.9 us (0.954)
  the two profiles are of different devices: /device:TPU:94 before, /device:TPU:89 now
where the time goes in v4:
time: 63.9 us; the launch traced here: 63.6 us
  Pallas kernels  56.4 us (88%)
  local copies, waits for them, and re-layouts  5.1 us (8%)
  other arithmetic  2.1 us (3%)
    pallas_call x1, Pallas kernels, window_attend(): pl.pallas_call(kernel, out_shape=jax.ShapeDtypeStruct((tok, qw), q.dtype)...  56.4 us
    unnamed x5, local copies, waits for them, and re-layouts  3.14 us
    convert_element_type x1, other arithmetic, shards(): rowok = (row_ids < own_count).astype(jnp.float32).reshape(tok_rows, 1)  1.33 us

profile of v4, /device:TPU:89, one launch (start us, length us, event | category | flops | bytes accessed | tf_op | source)
XLA Modules:
  0.0 63.6 jit_solution(10950634248000182751)
XLA Ops:
  0.0 0.0 copy-start
  0.0 0.7 %copy-done = s32[4,8,8]{2,1,0:T(8,128)S(1)} copy-done((s32[4,8,8]{2,1,0:T(8,128)S(1)}, s32[4,8,8]{2,1,0:T(8,128)}, u32[]{:S(2)}) %copy-start) | copy-done | bytes 1048
  0.7 0.7 %pad_dynamic-slice_fusion = s32[1,1,1]{2,1,0:T(1,128)} fusion(s32[]{:T(128)S(6)} %select_n.14, s32[]{:T(128)S(6)} %add.22, s32[]{:T(128)S(6)} %add.23, s32[4,8,8]{2,1,0:T(8,128)S(1)} %copy-done), kind=kLoop, calls=%fused_computation.2 | loop fusion | bytes 1040 | tf_op jit(solution)/shard_map/jit(dynamic_index_in_dim)/dynamic_slice | solution.py:282
  1.4 0.6 fusion.4
  1.9 0.7 %compare_bitcast_fusion = pred[4]{0:T(512)(128)(4,1)S(1)} fusion(s32[4,4]{1,0:T(4,128)} %param.9, s32[]{:T(128)S(6)} %select_n.14), kind=kLoop, calls=%fused_computation.17 | loop fusion | flops 4 | bytes 24 | tf_op jit(solution)/shard_map/gt | solution.py:284
  2.6 0.0 copy-start.1
  2.6 0.7 %copy-done.1 = s32[1,1,1,5]{3,2,1,0:T(1,128)S(1)} copy-done((s32[1,1,1,5]{3,2,1,0:T(1,128)S(1)}, s32[1,1,1,5]{3,2,1,0:T(1,128)}, u32[]{:S(2)}) %copy-start.1) | copy-done | bytes 44
  3.3 0.1 copy.7
  3.4 0.1 fusion.3
  3.5 0.6 reshape.93.refs_2_
  4.1 1.3 %fusion.refs_3_ = f32[128,1]{1,0:T(8,128)} fusion(s32[]{:T(128)} %bitcast.4), kind=kLoop, calls=%fused_computation.1 | loop fusion | flops 256 | bytes 516 | tf_op jit(solution)/shard_map/convert_element_type | solution.py:291
  5.4 56.4 %shard_map.55 = bf16[128,1536]{1,0:T(8,128)(2,1)} custom-call(bf16[128,1536]{1,0:T(8,128)(2,1)} %bitcast.19, bf16[128,1024]{1,0:T(8,128)(2,1)} %bitcast.20, f32[1,2560]{1,0:T(1,128)} %reshape.93.refs_2_, f32[128,1]{1,0:T(8,128)} %fusion.refs_3_), custom_call_target="tpu_custom_call" | custom-call | flops 2013265920 | bytes 6029312 | tf_op jit(solution)/shard_map/pallas_call | solution.py:249
  61.9 1.8 %copy.9 = bf16[1,1,1,128,1536]{4,3,2,1,0:T(8,128)(2,1)} copy(bf16[1,1,1,128,1536]{4,3,2,1,0:T(8,128)(2,1)} %bitcast.13) | data formatting | bytes 786432
  (2 shorter events, 0.0 us)
Async XLA Ops:
  0.0 0.7 %copy-start = (s32[4,8,8]{2,1,0:T(8,128)S(1)}, s32[4,8,8]{2,1,0:T(8,128)}, u32[]{:S(2)}) copy-start(s32[4,8,8]{2,1,0:T(8,128)} %param.8) | copy-start | bytes 3076
  2.6 0.7 %copy-start.1 = (s32[1,1,1,5]{3,2,1,0:T(1,128)S(1)}, s32[1,1,1,5]{3,2,1,0:T(1,128)}, u32[]{:S(2)}) copy-start(s32[1,1,1,5]{3,2,1,0:T(1,128)} %param.7) | copy-start | bytes 64

commit v5 on v4

--- a/solution.py
+++ b/solution.py
@@ -24,36 +24,47 @@
     )
 
 
-def attend_body(q_ref, kv_ref, live_ref, rowok_ref, o_ref):
-    kv_heads = kv_ref.shape[1] // (2 * HEAD_SIZE)
-    groups = q_ref.shape[1] // (kv_heads * HEAD_SIZE)
-    tok = q_ref.shape[0]
-    width = kv_heads * HEAD_SIZE
-    scale = HEAD_SIZE ** (-0.5)
-    live = live_ref[...] > 0
-    rowok = jnp.concatenate([rowok_ref[...]] * groups, axis=0) > 0
+def load_queries(q_ref, q3, kv_heads, groups):
     for h in range(kv_heads):
-        qh = jnp.concatenate(
+        q3[h] = jnp.concatenate(
             [q_ref[:, (h * groups + g) * HEAD_SIZE:(h * groups + g + 1) * HEAD_SIZE] for g in range(groups)],
             axis=0,
         )
-        kh = kv_ref[:, h * HEAD_SIZE:(h + 1) * HEAD_SIZE]
-        s = lax.dot_general(qh, kh, (((1,), (1,)), ((), ())), preferred_element_type=jnp.float32)
-        s = s * scale
-        s = jnp.where(live, s, -1e30)
-        m = jnp.max(s, axis=1, keepdims=True)
-        p = jnp.where(live, jnp.exp(s - m), 0.0)
-        tot = jnp.sum(p, axis=1, keepdims=True)
-        vh = kv_ref[:, width + h * HEAD_SIZE:width + (h + 1) * HEAD_SIZE]
-        acc = jnp.dot(p.astype(jnp.bfloat16), vh, preferred_element_type=jnp.float32)
-        res = jnp.where(rowok, acc / tot, 0.0).astype(o_ref.dtype)
+
+
+def attend_chunk(q3, kvbuf, live_ref, m_sc, l_sc, acc_sc, s, tok):
+    kv_heads = q3.shape[0]
+    width = kv_heads * HEAD_SIZE
+    scale = HEAD_SIZE ** (-0.5)
+    lo, n = s * NEIGH * tok, NEIGH * tok
+    live = live_ref[:, lo:lo + n] > 0
+    for h in range(kv_heads):
+        kh = kvbuf[lo:lo + n, h * HEAD_SIZE:(h + 1) * HEAD_SIZE]
+        sc = lax.dot_general(q3[h], kh, (((1,), (1,)), ((), ())), preferred_element_type=jnp.float32)
+        sc = jnp.where(live, sc * scale, -1e30)
+        m_old = m_sc[h]
+        m_new = jnp.maximum(m_old, jnp.max(sc, axis=1, keepdims=True))
+        p = jnp.where(live, jnp.exp(sc - m_new), 0.0)
+        fade = jnp.exp(m_old - m_new)
+        l_sc[h] = l_sc[h] * fade + jnp.sum(p, axis=1, keepdims=True)
+        vh = kvbuf[lo:lo + n, width + h * HEAD_SIZE:width + (h + 1) * HEAD_SIZE]
+        acc_sc[h] = acc_sc[h] * fade + jnp.dot(p.astype(jnp.bfloat16), vh, preferred_element_type=jnp.float32)
+        m_sc[h] = m_new
+
+
+def attend_finish(rowok_ref, l_sc, acc_sc, o_ref, groups, tok):
+    kv_heads = acc_sc.shape[0]
+    rowok = jnp.concatenate([rowok_ref[...]] * groups, axis=0) > 0
+    for h in range(kv_heads):
+        res = jnp.where(rowok, acc_sc[h] / l_sc[h], 0.0).astype(o_ref.dtype)
         for g in range(groups):
             col = (h * groups + g) * HEAD_SIZE
             o_ref[:, col:col + HEAD_SIZE] = res[g * tok:(g + 1) * tok]
 
 
 def window_kernel(spans, rows, cols, q_hbm, kv_ref, live_ref, rowok_ref, o_ref,
-                  q_ref, kvbuf, trans, send_sem, recv_sem, fwd_sem, trans_sem, local_sem):
+                  q_ref, kvbuf, trans, q3, m_sc, l_sc, acc_sc,
+                  send_sem, recv_sem, fwd_sem, trans_sem, local_sem):
     tok = kv_ref.shape[0]
     c = lax.axis_index("span")
     i = lax.axis_index("ty")
@@ -183,10 +194,6 @@
 
     zeros = jnp.zeros((tok, kv_ref.shape[1]), kv_ref.dtype)
     for s in range(spans):
-        @pl.when(s > c)
-        def _():
-            for o in range(NEIGH):
-                slot(s, o)[...] = zeros
         @pl.when(s <= c)
         def _():
             for d in range(1, NEIGH):
@@ -214,30 +221,42 @@
                 relay(s)
 
     for s in range(spans):
-        @pl.when(s <= c)
-        def _():
-            for o in range(1, NEIGH):
-                dy, dx = OFFSETS[o]
-                @pl.when(inside(o))
-                def _():
-                    pltpu.make_async_remote_copy(
-                        src_ref=kv_ref, dst_ref=slot(s, o), send_sem=send_sem.at[0],
-                        recv_sem=recv_sem.at[s * NEIGH + o],
-                        device_id=(c, i + dy, j + dx), device_id_type=mesh_id).wait_recv()
-
-    for s in range(spans):
         @pl.when(s > c)
         def _():
             up_copy(s).wait_send()
+    own.wait()
+    q_load.wait()
+
+    kv_heads = q3.shape[0]
+    groups = q_ref.shape[1] // (kv_heads * HEAD_SIZE)
+    load_queries(q_ref, q3, kv_heads, groups)
+    m_sc[...] = jnp.full(m_sc.shape, -1e30, jnp.float32)
+    l_sc[...] = jnp.zeros(l_sc.shape, jnp.float32)
+    acc_sc[...] = jnp.zeros(acc_sc.shape, jnp.float32)
+
+    for cc in range(spans):
+        @pl.when(c == cc)
+        def _():
+            order = [cc] + sorted(range(cc), key=lambda s: (ring_gap(s, cc), -s))
+            for s in order:
+                for o in range(1, NEIGH):
+                    dy, dx = OFFSETS[o]
+                    @pl.when(inside(o))
+                    def _():
+                        pltpu.make_async_remote_copy(
+                            src_ref=kv_ref, dst_ref=slot(s, o), send_sem=send_sem.at[0],
+                            recv_sem=recv_sem.at[s * NEIGH + o],
+                            device_id=(c, i + dy, j + dx), device_id_type=mesh_id).wait_recv()
+                attend_chunk(q3, kvbuf, live_ref, m_sc, l_sc, acc_sc, s, tok)
+
+    for s in range(spans):
         @pl.when(s <= c)
         def _():
             for d in range(1, NEIGH):
                 send_side(s, d, kv_ref, wait=True)
             relay(s, wait=True)
-    own.wait()
-    q_load.wait()
-
-    attend_body(q_ref, kvbuf, live_ref, rowok_ref, o_ref)
+
+    attend_finish(rowok_ref, l_sc, acc_sc, o_ref, groups, tok)
 
 
 def window_attend(q, kv, live, rowok, spans, rows, cols):
@@ -255,6 +274,10 @@
             pltpu.VMEM((tok, qw), q.dtype),
             pltpu.VMEM((keys, kw), kv.dtype),
             pltpu.VMEM((2, spans, tok, kw), kv.dtype),
+            pltpu.VMEM((kw // (2 * HEAD_SIZE), qw // (kw // 2) * tok, HEAD_SIZE), q.dtype),
+            pltpu.VMEM((kw // (2 * HEAD_SIZE), qw // (kw // 2) * tok, 1), jnp.float32),
+            pltpu.VMEM((kw // (2 * HEAD_SIZE), qw // (kw // 2) * tok, 1), jnp.float32),
+            pltpu.VMEM((kw // (2 * HEAD_SIZE), qw // (kw // 2) * tok, HEAD_SIZE), jnp.float32),
             pltpu.SemaphoreType.DMA((spans + spans * (NEIGH - 1),)),
             pltpu.SemaphoreType.DMA((spans * NEIGH,)),
             pltpu.SemaphoreType.DMA((2, spans)),

time: 63.9 us -> 61.8 us (0.967)
  the two profiles are of different devices: /device:TPU:89 before, /device:TPU:127 now
where the time goes in v5:
time: 61.8 us; the launch traced here: 61.5 us
  Pallas kernels  54.3 us (88%)
  local copies, waits for them, and re-layouts  5.1 us (8%)
  other arithmetic  2.1 us (3%)
    pallas_call x1, Pallas kernels, window_attend(): pl.pallas_call(kernel, out_shape=jax.ShapeDtypeStruct((tok, qw), q.dtype)...  54.3 us
    unnamed x5, local copies, waits for them, and re-layouts  3.14 us
    convert_element_type x1, other arithmetic, shards(): rowok = (row_ids < own_count).astype(jnp.float32).reshape(tok_rows, 1)  1.33 us

profile of v5, /device:TPU:127, one launch (start us, length us, event | category | flops | bytes accessed | tf_op | source)
XLA Modules:
  0.0 61.5 jit_solution(12436273924328160082)
XLA Ops:
  0.0 0.0 copy-start
  0.0 0.7 %copy-done = s32[4,8,8]{2,1,0:T(8,128)S(1)} copy-done((s32[4,8,8]{2,1,0:T(8,128)S(1)}, s32[4,8,8]{2,1,0:T(8,128)}, u32[]{:S(2)}) %copy-start) | copy-done | bytes 1048
  0.7 0.7 %pad_dynamic-slice_fusion = s32[1,1,1]{2,1,0:T(1,128)} fusion(s32[]{:T(128)S(6)} %select_n.14, s32[]{:T(128)S(6)} %add.22, s32[]{:T(128)S(6)} %add.23, s32[4,8,8]{2,1,0:T(8,128)S(1)} %copy-done), kind=kLoop, calls=%fused_computation.2 | loop fusion | bytes 1040 | tf_op jit(solution)/shard_map/jit(dynamic_index_in_dim)/dynamic_slice | solution.py:305
  1.4 0.6 fusion.4
  1.9 0.7 %compare_bitcast_fusion = pred[4]{0:T(512)(128)(4,1)S(1)} fusion(s32[4,4]{1,0:T(4,128)} %param.9, s32[]{:T(128)S(6)} %select_n.14), kind=kLoop, calls=%fused_computation.17 | loop fusion | flops 4 | bytes 24 | tf_op jit(solution)/shard_map/gt | solution.py:307
  2.6 0.0 copy-start.1
  2.6 0.7 %copy-done.1 = s32[1,1,1,5]{3,2,1,0:T(1,128)S(1)} copy-done((s32[1,1,1,5]{3,2,1,0:T(1,128)S(1)}, s32[1,1,1,5]{3,2,1,0:T(1,128)}, u32[]{:S(2)}) %copy-start.1) | copy-done | bytes 44
  3.3 0.1 copy.7
  3.4 0.1 fusion.3
  3.5 0.6 %reshape.93.refs_2_ = f32[1,2560]{1,0:T(1,128)} reshape(f32[4,5,128]{2,1,0:T(8,128)S(1)} %fusion.3) | data formatting | bytes 20480 | tf_op jit(solution)/shard_map/convert_element_type | solution.py:313
  4.1 1.3 %fusion.refs_3_ = f32[128,1]{1,0:T(8,128)} fusion(s32[]{:T(128)} %bitcast.4), kind=kLoop, calls=%fused_computation.1 | loop fusion | flops 256 | bytes 516 | tf_op jit(solution)/shard_map/convert_element_type | solution.py:314
  5.4 54.3 %shard_map.55 = bf16[128,1536]{1,0:T(8,128)(2,1)} custom-call(bf16[128,1536]{1,0:T(8,128)(2,1)} %bitcast.19, bf16[128,1024]{1,0:T(8,128)(2,1)} %bitcast.20, f32[1,2560]{1,0:T(1,128)} %reshape.93.refs_2_, f32[128,1]{1,0:T(8,128)} %fusion.refs_3_), custom_call_target="tpu_custom_call" | custom-call | flops 2013265920 | bytes 6029312 | tf_op jit(solution)/shard_map/pallas_call | solution.py:268
  59.7 1.8 %copy.9 = bf16[1,1,1,128,1536]{4,3,2,1,0:T(8,128)(2,1)} copy(bf16[1,1,1,128,1536]{4,3,2,1,0:T(8,128)(2,1)} %bitcast.13) | data formatting | bytes 786432
  (2 shorter events, 0.0 us)
Async XLA Ops:
  0.0 0.7 %copy-start = (s32[4,8,8]{2,1,0:T(8,128)S(1)}, s32[4,8,8]{2,1,0:T(8,128)}, u32[]{:S(2)}) copy-start(s32[4,8,8]{2,1,0:T(8,128)} %param.8) | copy-start | bytes 3076
  2.6 0.7 %copy-start.1 = (s32[1,1,1,5]{3,2,1,0:T(1,128)S(1)}, s32[1,1,1,5]{3,2,1,0:T(1,128)}, u32[]{:S(2)}) copy-start(s32[1,1,1,5]{3,2,1,0:T(1,128)} %param.7) | copy-start | bytes 64

commit v6 on v5

--- a/solution.py
+++ b/solution.py
@@ -218,6 +218,7 @@
                     device_id=(s, i, j), device_id_type=mesh_id).wait_recv()
                 for d in range(1, NEIGH):
                     send_side(s, d, slot(s, 0))
+            for s in sorted(range(cc), key=lambda s: (ring_gap(s, cc), -s)):
                 relay(s)
 
     for s in range(spans):

time: 61.8 us -> 64.1 us (1.037)
  the two profiles are of different devices: /device:TPU:127 before, /device:TPU:88 now
where the time goes in v6:
time: 64.1 us; the launch traced here: 63.9 us
  Pallas kernels  56.7 us (88%)
  local copies, waits for them, and re-layouts  5.1 us (8%)
  other arithmetic  2.1 us (3%)
    pallas_call x1, Pallas kernels, window_attend(): pl.pallas_call(kernel, out_shape=jax.ShapeDtypeStruct((tok, qw), q.dtype)...  56.7 us
    unnamed x5, local copies, waits for them, and re-layouts  3.14 us
    convert_element_type x1, other arithmetic, shards(): rowok = (row_ids < own_count).astype(jnp.float32).reshape(tok_rows, 1)  1.33 us

profile of v6, /device:TPU:88, one launch (start us, length us, event | category | flops | bytes accessed | tf_op | source)
XLA Modules:
  0.0 63.9 jit_solution(13091351898247826985)
XLA Ops:
  0.0 0.0 copy-start
  0.0 0.7 %copy-done = s32[4,8,8]{2,1,0:T(8,128)S(1)} copy-done((s32[4,8,8]{2,1,0:T(8,128)S(1)}, s32[4,8,8]{2,1,0:T(8,128)}, u32[]{:S(2)}) %copy-start) | copy-done | bytes 1048
  0.7 0.7 %pad_dynamic-slice_fusion = s32[1,1,1]{2,1,0:T(1,128)} fusion(s32[]{:T(128)S(6)} %select_n.14, s32[]{:T(128)S(6)} %add.22, s32[]{:T(128)S(6)} %add.23, s32[4,8,8]{2,1,0:T(8,128)S(1)} %copy-done), kind=kLoop, calls=%fused_computation.2 | loop fusion | bytes 1040 | tf_op jit(solution)/shard_map/jit(dynamic_index_in_dim)/dynamic_slice | solution.py:306
  1.4 0.6 fusion.4
  1.9 0.7 %compare_bitcast_fusion = pred[4]{0:T(512)(128)(4,1)S(1)} fusion(s32[4,4]{1,0:T(4,128)} %param.9, s32[]{:T(128)S(6)} %select_n.14), kind=kLoop, calls=%fused_computation.17 | loop fusion | flops 4 | bytes 24 | tf_op jit(solution)/shard_map/gt | solution.py:308
  2.6 0.0 copy-start.1
  2.6 0.7 %copy-done.1 = s32[1,1,1,5]{3,2,1,0:T(1,128)S(1)} copy-done((s32[1,1,1,5]{3,2,1,0:T(1,128)S(1)}, s32[1,1,1,5]{3,2,1,0:T(1,128)}, u32[]{:S(2)}) %copy-start.1) | copy-done | bytes 44
  3.3 0.1 copy.7
  3.4 0.1 fusion.3
  3.5 0.6 reshape.93.refs_2_
  4.1 1.3 %fusion.refs_3_ = f32[128,1]{1,0:T(8,128)} fusion(s32[]{:T(128)} %bitcast.4), kind=kLoop, calls=%fused_computation.1 | loop fusion | flops 256 | bytes 516 | tf_op jit(solution)/shard_map/convert_element_type | solution.py:315
  5.4 56.7 %shard_map.55 = bf16[128,1536]{1,0:T(8,128)(2,1)} custom-call(bf16[128,1536]{1,0:T(8,128)(2,1)} %bitcast.19, bf16[128,1024]{1,0:T(8,128)(2,1)} %bitcast.20, f32[1,2560]{1,0:T(1,128)} %reshape.93.refs_2_, f32[128,1]{1,0:T(8,128)} %fusion.refs_3_), custom_call_target="tpu_custom_call" | custom-call | flops 2013265920 | bytes 6029312 | tf_op jit(solution)/shard_map/pallas_call | solution.py:269
  62.1 1.8 %copy.9 = bf16[1,1,1,128,1536]{4,3,2,1,0:T(8,128)(2,1)} copy(bf16[1,1,1,128,1536]{4,3,2,1,0:T(8,128)(2,1)} %bitcast.13) | data formatting | bytes 786432
  (2 shorter events, 0.0 us)
Async XLA Ops:
  0.0 0.7 %copy-start = (s32[4,8,8]{2,1,0:T(8,128)S(1)}, s32[4,8,8]{2,1,0:T(8,128)}, u32[]{:S(2)}) copy-start(s32[4,8,8]{2,1,0:T(8,128)} %param.8) | copy-start | bytes 3076
  2.6 0.7 %copy-start.1 = (s32[1,1,1,5]{3,2,1,0:T(1,128)S(1)}, s32[1,1,1,5]{3,2,1,0:T(1,128)}, u32[]{:S(2)}) copy-start(s32[1,1,1,5]{3,2,1,0:T(1,128)} %param.7) | copy-start | bytes 64

commit v7 on v5

--- a/solution.py
+++ b/solution.py
@@ -63,20 +63,17 @@
 
 
 def window_kernel(spans, rows, cols, q_hbm, kv_ref, live_ref, rowok_ref, o_ref,
-                  q_ref, kvbuf, trans, q3, m_sc, l_sc, acc_sc,
-                  send_sem, recv_sem, fwd_sem, trans_sem, local_sem):
+                  q_ref, kvbuf, q3, m_sc, l_sc, acc_sc,
+                  send_sem, recv_sem, lift_sem, local_sem):
     tok = kv_ref.shape[0]
     c = lax.axis_index("span")
     i = lax.axis_index("ty")
     j = lax.axis_index("tx")
     mesh_id = pl.DeviceIdType.MESH
-    relayed = cols >= 4
+    lifted = cols >= 4
     half = cols // 2
     is_a = j == half - 1
     is_b = j == half
-
-    def relay_col(s):
-        return 0 if s % 2 == 0 else cols - 1
 
     def inside(d):
         dy, dx = OFFSETS[d]
@@ -86,14 +83,12 @@
     def slot(s, o):
         return kvbuf.at[pl.ds((s * NEIGH + o) * tok, tok), :]
 
-    def boundary(d):
-        if not relayed or d not in (3, 4):
+    def crossing(d):
+        if not lifted or d not in (3, 4):
             return None
         return is_a if d == 4 else is_b
 
     n_nb = sum(inside(d).astype(jnp.int32) for d in range(1, NEIGH))
-    ends = (is_a | is_b | (j == 0) | (j == cols - 1)) if relayed else (j < 0)
-    n_extra = jnp.where(ends, 2, 0)
 
     barrier = pltpu.get_barrier_semaphore()
     def greet(target):
@@ -107,16 +102,7 @@
         @pl.when(inside(d))
         def _():
             greet((c, i + dy, j + dx))
-    if relayed:
-        @pl.when(is_a | is_b)
-        def _():
-            greet((c, i, 0))
-            greet((c, i, cols - 1))
-        @pl.when((j == 0) | (j == cols - 1))
-        def _():
-            greet((c, i, half - 1))
-            greet((c, i, half))
-    pl.semaphore_wait(barrier, spans - 1 + n_nb + n_extra)
+    pl.semaphore_wait(barrier, spans - 1 + n_nb)
 
     def up_copy(s):
         return pltpu.make_async_remote_copy(
@@ -131,46 +117,19 @@
             recv_sem=recv_sem.at[s * NEIGH + INVERSE[d]],
             device_id=(c, i + dy, j + dx), device_id_type=mesh_id)
 
-    def to_relay(s, d, src):
-        way = 0 if d == 4 else 1
+    def lift_copy(s, o):
         return pltpu.make_async_remote_copy(
-            src_ref=src, dst_ref=trans.at[way, s],
-            send_sem=send_sem.at[spans + s * (NEIGH - 1) + d - 1],
-            recv_sem=trans_sem.at[way, s],
-            device_id=(c, i, relay_col(s)), device_id_type=mesh_id)
-
-    def from_relay(s, way):
-        target = half if way == 0 else half - 1
-        o = 3 if way == 0 else 4
-        return pltpu.make_async_remote_copy(
-            src_ref=trans.at[way, s], dst_ref=slot(s, o),
-            send_sem=fwd_sem.at[way, s], recv_sem=recv_sem.at[s * NEIGH + o],
-            device_id=(c, i, target), device_id_type=mesh_id)
-
-    def send_side(s, d, src, wait=False):
-        bnd = boundary(d)
-        direct = inside(d) if bnd is None else inside(d) & jnp.logical_not(bnd)
-        @pl.when(direct)
+            src_ref=slot(c, o), dst_ref=slot(c, o), send_sem=lift_sem.at[s],
+            recv_sem=recv_sem.at[c * NEIGH + o],
+            device_id=(s, i, j), device_id_type=mesh_id)
+
+    def send_side(s, d, src, wait=False, own=False):
+        cross = crossing(d)
+        go = inside(d) if (cross is None or own) else inside(d) & jnp.logical_not(cross)
+        @pl.when(go)
         def _():
             cp = side_copy(s, d, src)
             cp.wait_send() if wait else cp.start()
-        if bnd is not None:
-            @pl.when(bnd)
-            def _():
-                cp = to_relay(s, d, src)
-                cp.wait_send() if wait else cp.start()
-
-    def relay(s, wait=False):
-        if not relayed:
-            return
-        @pl.when(j == relay_col(s))
-        def _():
-            for way in (0, 1):
-                if wait:
-                    from_relay(s, way).wait_send()
-                else:
-                    to_relay(s, 4 if way == 0 else 3, kv_ref).wait_recv()
-                    from_relay(s, way).start()
 
     q_load = pltpu.make_async_copy(q_hbm, q_ref, local_sem.at[1])
     q_load.start()
@@ -184,13 +143,30 @@
         @pl.when(s == c)
         def _():
             for d in range(1, NEIGH):
-                send_side(s, d, kv_ref)
+                send_side(s, d, kv_ref, own=True)
 
     own = pltpu.make_async_copy(kv_ref, slot(0, 0), local_sem.at[0])
     for s in range(spans):
         @pl.when(s == c)
         def _():
             pltpu.make_async_copy(kv_ref, slot(s, 0), local_sem.at[0]).start()
+
+    if lifted:
+        for o, end in ((4, is_a), (3, is_b)):
+            dy, dx = OFFSETS[o]
+            @pl.when(end)
+            def _():
+                for s in range(spans):
+                    @pl.when(s == c)
+                    def _():
+                        pltpu.make_async_remote_copy(
+                            src_ref=kv_ref, dst_ref=slot(s, o), send_sem=send_sem.at[0],
+                            recv_sem=recv_sem.at[s * NEIGH + o],
+                            device_id=(c, i + dy, j + dx), device_id_type=mesh_id).wait_recv()
+                for s in range(spans):
+                    @pl.when(s > c)
+                    def _():
+                        lift_copy(s, o).start()
 
     zeros = jnp.zeros((tok, kv_ref.shape[1]), kv_ref.dtype)
     for s in range(spans):
@@ -200,11 +176,6 @@
                 @pl.when(jnp.logical_not(inside(INVERSE[d])))
                 def _():
                     slot(s, INVERSE[d])[...] = zeros
-
-    for s in range(spans):
-        @pl.when(s == c)
-        def _():
-            relay(s)
 
     def ring_gap(a, b):
         return min((a - b) % spans, (b - a) % spans)
@@ -218,7 +189,6 @@
                     device_id=(s, i, j), device_id_type=mesh_id).wait_recv()
                 for d in range(1, NEIGH):
                     send_side(s, d, slot(s, 0))
-                relay(s)
 
     for s in range(spans):
         @pl.when(s > c)
@@ -241,7 +211,10 @@
             for s in order:
                 for o in range(1, NEIGH):
                     dy, dx = OFFSETS[o]
-                    @pl.when(inside(o))
+                    done = inside(o)
+                    if lifted and s == cc and o in (3, 4):
+                        done = done & jnp.logical_not(is_a if o == 4 else is_b)
+                    @pl.when(done)
                     def _():
                         pltpu.make_async_remote_copy(
                             src_ref=kv_ref, dst_ref=slot(s, o), send_sem=send_sem.at[0],
@@ -249,12 +222,18 @@
                             device_id=(c, i + dy, j + dx), device_id_type=mesh_id).wait_recv()
                 attend_chunk(q3, kvbuf, live_ref, m_sc, l_sc, acc_sc, s, tok)
 
-    for s in range(spans):
-        @pl.when(s <= c)
-        def _():
-            for d in range(1, NEIGH):
-                send_side(s, d, kv_ref, wait=True)
-            relay(s, wait=True)
+    for cc in range(spans):
+        @pl.when(c == cc)
+        def _():
+            for s in range(cc + 1):
+                for d in range(1, NEIGH):
+                    send_side(s, d, kv_ref, wait=True, own=(s == cc))
+            if lifted:
+                for o, end in ((4, is_a), (3, is_b)):
+                    @pl.when(end)
+                    def _():
+                        for s in range(cc + 1, spans):
+                            lift_copy(s, o).wait_send()
 
     attend_finish(rowok_ref, l_sc, acc_sc, o_ref, groups, tok)
 
@@ -273,15 +252,13 @@
         scratch_shapes=[
             pltpu.VMEM((tok, qw), q.dtype),
             pltpu.VMEM((keys, kw), kv.dtype),
-            pltpu.VMEM((2, spans, tok, kw), kv.dtype),
             pltpu.VMEM((kw // (2 * HEAD_SIZE), qw // (kw // 2) * tok, HEAD_SIZE), q.dtype),
             pltpu.VMEM((kw // (2 * HEAD_SIZE), qw // (kw // 2) * tok, 1), jnp.float32),
             pltpu.VMEM((kw // (2 * HEAD_SIZE), qw // (kw // 2) * tok, 1), jnp.float32),
             pltpu.VMEM((kw // (2 * HEAD_SIZE), qw // (kw // 2) * tok, HEAD_SIZE), jnp.float32),
             pltpu.SemaphoreType.DMA((spans + spans * (NEIGH - 1),)),
             pltpu.SemaphoreType.DMA((spans * NEIGH,)),
-            pltpu.SemaphoreType.DMA((2, spans)),
-            pltpu.SemaphoreType.DMA((2, spans)),
+            pltpu.SemaphoreType.DMA((spans,)),
             pltpu.SemaphoreType.DMA((2,)),
         ],
         compiler_params=pltpu.CompilerParams(

time: 61.8 us -> 52.1 us (0.84)
  the two profiles are of different devices: /device:TPU:127 before, /device:TPU:95 now
where the time goes in v7:
time: 52.1 us; the launch traced here: 51.8 us
  Pallas kernels  44.6 us (86%)
  local copies, waits for them, and re-layouts  5.1 us (10%)
  other arithmetic  2.1 us (4%)
    pallas_call x1, Pallas kernels, window_attend(): pl.pallas_call(kernel, out_shape=jax.ShapeDtypeStruct((tok, qw), q.dtype)...  44.6 us
    unnamed x5, local copies, waits for them, and re-layouts  3.14 us
    convert_element_type x1, other arithmetic, shards(): rowok = (row_ids < own_count).astype(jnp.float32).reshape(tok_rows, 1)  1.33 us

profile of v7, /device:TPU:95, one launch (start us, length us, event | category | flops | bytes accessed | tf_op | source)
XLA Modules:
  0.0 51.8 jit_solution(13610143219219760727)
XLA Ops:
  0.0 0.0 copy-start
  0.0 0.7 %copy-done = s32[4,8,8]{2,1,0:T(8,128)S(1)} copy-done((s32[4,8,8]{2,1,0:T(8,128)S(1)}, s32[4,8,8]{2,1,0:T(8,128)}, u32[]{:S(2)}) %copy-start) | copy-done | bytes 1048
  0.7 0.7 %pad_dynamic-slice_fusion = s32[1,1,1]{2,1,0:T(1,128)} fusion(s32[]{:T(128)S(6)} %select_n.14, s32[]{:T(128)S(6)} %add.22, s32[]{:T(128)S(6)} %add.23, s32[4,8,8]{2,1,0:T(8,128)S(1)} %copy-done), kind=kLoop, calls=%fused_computation.2 | loop fusion | bytes 1040 | tf_op jit(solution)/shard_map/jit(dynamic_index_in_dim)/dynamic_slice | solution.py:282
  1.4 0.6 %fusion.4 = (s32[4]{0:T(128)S(1)}, s32[4]{0:T(128)S(1)}, s32[4]{0:T(128)S(1)}, s32[4]{0:T(128)S(1)}, s32[4]{0:T(128)S(1)}) fusion(s32[]{:T(128)S(6)} %add.22, s32[]{:T(128)S(6)} %add.29, s32[4,8,8]{2,1,0:T(8,128)S(1)} %copy-done, s32[]{:T(128)S(6)} %select_n.12, s32[]{:T(128)S(6)} %add.23, s32[]{:T(128)S(6)} %add.25, s32[]{:T(128)S(6)} %select_n.13), kind=kLoop, calls=%fused_computation.12 | loop fusion | bytes 1128 | tf_op jit(solution)/shard_map/slice | solution.py:21
  1.9 0.7 %compare_bitcast_fusion = pred[4]{0:T(512)(128)(4,1)S(1)} fusion(s32[4,4]{1,0:T(4,128)} %param.9, s32[]{:T(128)S(6)} %select_n.14), kind=kLoop, calls=%fused_computation.17 | loop fusion | flops 4 | bytes 24 | tf_op jit(solution)/shard_map/gt | solution.py:284
  2.6 0.0 copy-start.1
  2.6 0.7 %copy-done.1 = s32[1,1,1,5]{3,2,1,0:T(1,128)S(1)} copy-done((s32[1,1,1,5]{3,2,1,0:T(1,128)S(1)}, s32[1,1,1,5]{3,2,1,0:T(1,128)}, u32[]{:S(2)}) %copy-start.1) | copy-done | bytes 44
  3.3 0.1 copy.7
  3.4 0.1 fusion.3
  3.5 0.6 %reshape.93.refs_2_ = f32[1,2560]{1,0:T(1,128)} reshape(f32[4,5,128]{2,1,0:T(8,128)S(1)} %fusion.3) | data formatting | bytes 20480 | tf_op jit(solution)/shard_map/convert_element_type | solution.py:290
  4.1 1.3 %fusion.refs_3_ = f32[128,1]{1,0:T(8,128)} fusion(s32[]{:T(128)} %bitcast.4), kind=kLoop, calls=%fused_computation.1 | loop fusion | flops 256 | bytes 516 | tf_op jit(solution)/shard_map/convert_element_type | solution.py:291
  5.4 44.6 %shard_map.55 = bf16[128,1536]{1,0:T(8,128)(2,1)} custom-call(bf16[128,1536]{1,0:T(8,128)(2,1)} %bitcast.19, bf16[128,1024]{1,0:T(8,128)(2,1)} %bitcast.20, f32[1,2560]{1,0:T(1,128)} %reshape.93.refs_2_, f32[128,1]{1,0:T(8,128)} %fusion.refs_3_), custom_call_target="tpu_custom_call" | custom-call | flops 2013265920 | bytes 6029312 | tf_op jit(solution)/shard_map/pallas_call | solution.py:247
  50.1 1.8 %copy.9 = bf16[1,1,1,128,1536]{4,3,2,1,0:T(8,128)(2,1)} copy(bf16[1,1,1,128,1536]{4,3,2,1,0:T(8,128)(2,1)} %bitcast.13) | data formatting | bytes 786432
  (2 shorter events, 0.0 us)
Async XLA Ops:
  0.0 0.7 %copy-start = (s32[4,8,8]{2,1,0:T(8,128)S(1)}, s32[4,8,8]{2,1,0:T(8,128)}, u32[]{:S(2)}) copy-start(s32[4,8,8]{2,1,0:T(8,128)} %param.8) | copy-start | bytes 3076
  2.6 0.7 %copy-start.1 = (s32[1,1,1,5]{3,2,1,0:T(1,128)S(1)}, s32[1,1,1,5]{3,2,1,0:T(1,128)}, u32[]{:S(2)}) copy-start(s32[1,1,1,5]{3,2,1,0:T(1,128)} %param.7) | copy-start | bytes 64

commit v8 on v7

--- a/solution.py
+++ b/solution.py
@@ -32,12 +32,17 @@
         )
 
 
-def attend_chunk(q3, kvbuf, live_ref, m_sc, l_sc, acc_sc, s, tok):
+def attend_chunk(q3, kvbuf, limits, m_sc, l_sc, acc_sc, s, tok):
     kv_heads = q3.shape[0]
     width = kv_heads * HEAD_SIZE
     scale = HEAD_SIZE ** (-0.5)
     lo, n = s * NEIGH * tok, NEIGH * tok
-    live = live_ref[:, lo:lo + n] > 0
+    lane = lax.broadcasted_iota(jnp.int32, (1, n), 1)
+    block = lane // tok
+    limit = jnp.full((1, n), limits[NEIGH - 1], jnp.int32)
+    for o in range(NEIGH - 2, -1, -1):
+        limit = jnp.where(block == o, limits[o], limit)
+    live = (lane % tok) < limit
     for h in range(kv_heads):
         kh = kvbuf[lo:lo + n, h * HEAD_SIZE:(h + 1) * HEAD_SIZE]
         sc = lax.dot_general(q3[h], kh, (((1,), (1,)), ((), ())), preferred_element_type=jnp.float32)
@@ -52,9 +57,9 @@
         m_sc[h] = m_new
 
 
-def attend_finish(rowok_ref, l_sc, acc_sc, o_ref, groups, tok):
+def attend_finish(own_count, l_sc, acc_sc, o_ref, groups, tok):
     kv_heads = acc_sc.shape[0]
-    rowok = jnp.concatenate([rowok_ref[...]] * groups, axis=0) > 0
+    rowok = (lax.broadcasted_iota(jnp.int32, (groups * tok, 1), 0) % tok) < own_count
     for h in range(kv_heads):
         res = jnp.where(rowok, acc_sc[h] / l_sc[h], 0.0).astype(o_ref.dtype)
         for g in range(groups):
@@ -62,7 +67,7 @@
             o_ref[:, col:col + HEAD_SIZE] = res[g * tok:(g + 1) * tok]
 
 
-def window_kernel(spans, rows, cols, q_hbm, kv_ref, live_ref, rowok_ref, o_ref,
+def window_kernel(spans, rows, cols, q_hbm, kv_ref, counts_ref, pattern_ref, mask_ref, o_ref,
                   q_ref, kvbuf, q3, m_sc, l_sc, acc_sc,
                   send_sem, recv_sem, lift_sem, local_sem):
     tok = kv_ref.shape[0]
@@ -89,6 +94,17 @@
         return is_a if d == 4 else is_b
 
     n_nb = sum(inside(d).astype(jnp.int32) for d in range(1, NEIGH))
+
+    def window_limits(s):
+        reads = mask_ref[c, s] > 0
+        limits = []
+        for o in range(NEIGH):
+            dy, dx = OFFSETS[o]
+            y = jnp.minimum(jnp.maximum(i + dy, 0), rows - 1)
+            x = jnp.minimum(jnp.maximum(j + dx, 0), cols - 1)
+            ok = inside(o) & reads & (pattern_ref[0, 0, 0, o] > 0)
+            limits.append(jnp.where(ok, counts_ref[s, y, x], 0))
+        return limits
 
     barrier = pltpu.get_barrier_semaphore()
     def greet(target):
@@ -220,7 +236,7 @@
                             src_ref=kv_ref, dst_ref=slot(s, o), send_sem=send_sem.at[0],
                             recv_sem=recv_sem.at[s * NEIGH + o],
                             device_id=(c, i + dy, j + dx), device_id_type=mesh_id).wait_recv()
-                attend_chunk(q3, kvbuf, live_ref, m_sc, l_sc, acc_sc, s, tok)
+                attend_chunk(q3, kvbuf, window_limits(s), m_sc, l_sc, acc_sc, s, tok)
 
     for cc in range(spans):
         @pl.when(c == cc)
@@ -235,19 +251,20 @@
                         for s in range(cc + 1, spans):
                             lift_copy(s, o).wait_send()
 
-    attend_finish(rowok_ref, l_sc, acc_sc, o_ref, groups, tok)
-
-
-def window_attend(q, kv, live, rowok, spans, rows, cols):
+    attend_finish(counts_ref[c, i, j], l_sc, acc_sc, o_ref, groups, tok)
+
+
+def window_attend(q, kv, pattern, counts, span_mask):
     tok, qw = q.shape
     kw = kv.shape[1]
+    spans, rows, cols = counts.shape
     keys = spans * NEIGH * tok
     flops = 2 * 2 * tok * qw * keys
     kernel = lambda *refs: window_kernel(spans, rows, cols, *refs)
     return pl.pallas_call(
         kernel,
         out_shape=jax.ShapeDtypeStruct((tok, qw), q.dtype),
-        in_specs=[pl.BlockSpec(memory_space=pl.ANY)] * 2 + [pl.BlockSpec(memory_space=pltpu.VMEM)] * 2,
+        in_specs=[pl.BlockSpec(memory_space=pl.ANY)] * 2 + [pl.BlockSpec(memory_space=pltpu.SMEM)] * 3,
         out_specs=pl.BlockSpec(memory_space=pltpu.VMEM),
         scratch_shapes=[
             pltpu.VMEM((tok, qw), q.dtype),
@@ -266,31 +283,13 @@
         cost_estimate=pl.CostEstimate(
             flops=flops, transcendentals=tok * qw // HEAD_SIZE * keys,
             bytes_accessed=2 * (2 * tok * qw + keys * kw)),
-    )(q, kv, live, rowok)
+    )(q, kv, counts, pattern, span_mask)
 
 
 def shards(queries, key_value, pattern, counts, span_mask):
     tok_rows = queries.shape[3]
-    spans, rows, cols = counts.shape
-    my_span = lax.axis_index("span")
-    my_row = lax.axis_index("ty")
-    my_col = lax.axis_index("tx")
-    zero_index = jnp.asarray(0).astype(jnp.int32)
-    padded_counts = jnp.pad(counts, ((0, 0), (1, 1), (1, 1)))
-    window = lax.dynamic_slice(padded_counts, (zero_index, my_row, my_col), (spans, 3, 3))
-    near_counts = cross_tiles(window)
-    own_count = lax.dynamic_index_in_dim(window[:, 1, 1], my_span, 0, keepdims=False)
-    allowed = pattern.reshape(NEIGH) > 0
-    span_row = lax.dynamic_index_in_dim(span_mask, my_span, 0, keepdims=False) > 0
-    row_ids = jnp.arange(tok_rows, dtype=jnp.int32)
-    live = (
-        (row_ids[None, None, :] < near_counts[:, :, None])
-        & allowed[None, :, None]
-        & span_row[:, None, None]
-    ).reshape(1, -1).astype(jnp.float32)
-    rowok = (row_ids < own_count).astype(jnp.float32).reshape(tok_rows, 1)
     out = window_attend(
-        queries.reshape(tok_rows, -1), key_value.reshape(tok_rows, -1), live, rowok, spans, rows, cols)
+        queries.reshape(tok_rows, -1), key_value.reshape(tok_rows, -1), pattern, counts, span_mask)
     return out.reshape(1, 1, 1, tok_rows, -1)
 
 

time: 52.1 us -> 46.7 us (0.90)
  local copies, waits for them, and re-layouts: 5.1 us -> 1.77 us
  other arithmetic: 2.1 us -> 0 us
    convert_element_type x2 -> x0, other arithmetic: 1.4 us -> none  [the longest x1 1.33 us: shards(): rowok = (row_ids < own_count).astype(jnp.float32).reshape(tok_rows, 1)]
    unnamed x5 -> x1, local copies, waits for them, and re-layouts: 3.14 us -> 1.77 us
    gt x2 -> x0, other arithmetic: 0.7 us -> none  [the longest x1 0.69 us: shards(): lax.dynamic_index_in_dim(span_mask, my_span, 0, keepdims=False) > 0]
    dynamic_slice x1 -> x0, local copies, waits for them, and re-layouts: 0.67 us -> none  [shards(): lax.dynamic_index_in_dim(window[:, 1, 1], my_span, 0, keepdims=False)]
    convert_element_type x1 -> x0, local copies, waits for them, and re-layouts: 0.62 us -> none  [shards(): live = ((row_ids[None, None, :] < near_counts[:, :, None]) & allowed[None...]
    slice x1 -> x0, local copies, waits for them, and re-layouts: 0.56 us -> none  [cross_tiles(): extended[:, 1, 2]]
where the time goes in v8:
time: 46.7 us; the launch traced here: 46.5 us
  Pallas kernels  44.7 us (96%)
  local copies, waits for them, and re-layouts  1.77 us (4%)
    pallas_call x1, Pallas kernels, window_attend(): pl.pallas_call(kernel, out_shape=jax.ShapeDtypeStruct((tok, qw), q.dtype)...  44.7 us
    unnamed x1, local copies, waits for them, and re-layouts  1.77 us

profile of v8, /device:TPU:95, one launch (start us, length us, event | category | flops | bytes accessed | tf_op | source)
XLA Modules:
  0.0 46.5 jit_solution(12188303842761899211)
XLA Ops:
  0.0 44.7 %shard_map.55 = bf16[128,1536]{1,0:T(8,128)(2,1)} custom-call(bf16[128,1536]{1,0:T(8,128)(2,1)} %bitcast.4, bf16[128,1024]{1,0:T(8,128)(2,1)} %bitcast.5, s32[4,8,8]{2,1,0:T(8,128)} %refs_2_.1, s32[1,1,1,5]{3,2,1,0:T(1,128)} %refs_3_.1, s32[4,4]{1,0:T(4,128)} %refs_4_.1), custom_call_target="tpu_custom_call" | custom-call | flops 2013265920 | bytes 6029312 | tf_op jit(solution)/shard_map/pallas_call | solution.py:264
  44.8 1.8 %copy.7 = bf16[1,1,1,128,1536]{4,3,2,1,0:T(8,128)(2,1)} copy(bf16[1,1,1,128,1536]{4,3,2,1,0:T(8,128)(2,1)} %bitcast.3) | data formatting | bytes 786432

commit v9 on v8

--- a/solution.py
+++ b/solution.py
@@ -67,8 +67,8 @@
             o_ref[:, col:col + HEAD_SIZE] = res[g * tok:(g + 1) * tok]
 
 
-def window_kernel(spans, rows, cols, q_hbm, kv_ref, counts_ref, pattern_ref, mask_ref, o_ref,
-                  q_ref, kvbuf, q3, m_sc, l_sc, acc_sc,
+def window_kernel(spans, rows, cols, q_hbm, kv_ref, counts_ref, pattern_ref, mask_ref, o_hbm,
+                  q_ref, o_ref, kvbuf, q3, m_sc, l_sc, acc_sc,
                   send_sem, recv_sem, lift_sem, local_sem):
     tok = kv_ref.shape[0]
     c = lax.axis_index("span")
@@ -252,6 +252,9 @@
                             lift_copy(s, o).wait_send()
 
     attend_finish(counts_ref[c, i, j], l_sc, acc_sc, o_ref, groups, tok)
+    store = pltpu.make_async_copy(o_ref, o_hbm, local_sem.at[1])
+    store.start()
+    store.wait()
 
 
 def window_attend(q, kv, pattern, counts, span_mask):
@@ -265,8 +268,9 @@
         kernel,
         out_shape=jax.ShapeDtypeStruct((tok, qw), q.dtype),
         in_specs=[pl.BlockSpec(memory_space=pl.ANY)] * 2 + [pl.BlockSpec(memory_space=pltpu.SMEM)] * 3,
-        out_specs=pl.BlockSpec(memory_space=pltpu.VMEM),
+        out_specs=pl.BlockSpec(memory_space=pl.ANY),
         scratch_shapes=[
+            pltpu.VMEM((tok, qw), q.dtype),
             pltpu.VMEM((tok, qw), q.dtype),
             pltpu.VMEM((keys, kw), kv.dtype),
             pltpu.VMEM((kw // (2 * HEAD_SIZE), qw // (kw // 2) * tok, HEAD_SIZE), q.dtype),

time: 46.7 us -> 46.7 us (level)
  no operation moved by 1% of the time
where the time goes in v9:
time: 46.7 us; the launch traced here: 46.5 us
  Pallas kernels  44.7 us (96%)
  local copies, waits for them, and re-layouts  1.77 us (4%)
    pallas_call x1, Pallas kernels, window_attend(): pl.pallas_call(kernel, out_shape=jax.ShapeDtypeStruct((tok, qw), q.dtype)...  44.7 us
    unnamed x1, local copies, waits for them, and re-layouts  1.77 us

profile of v9, /device:TPU:95, one launch (start us, length us, event | category | flops | bytes accessed | tf_op | source)
XLA Modules:
  0.0 46.5 jit_solution(3347783712137342630)
XLA Ops:
  0.0 44.7 %shard_map.55 = bf16[128,1536]{1,0:T(8,128)(2,1)} custom-call(bf16[128,1536]{1,0:T(8,128)(2,1)} %bitcast.4, bf16[128,1024]{1,0:T(8,128)(2,1)} %bitcast.5, s32[4,8,8]{2,1,0:T(8,128)} %refs_2_.1, s32[1,1,1,5]{3,2,1,0:T(1,128)} %refs_3_.1, s32[4,4]{1,0:T(4,128)} %refs_4_.1), custom_call_target="tpu_custom_call" | custom-call | flops 2013265920 | bytes 6029312 | tf_op jit(solution)/shard_map/pallas_call | solution.py:267
  44.7 1.8 %copy.7 = bf16[1,1,1,128,1536]{4,3,2,1,0:T(8,128)(2,1)} copy(bf16[1,1,1,128,1536]{4,3,2,1,0:T(8,128)(2,1)} %bitcast.3) | data formatting | bytes 786432

commit v10 on v9

--- a/solution.py
+++ b/solution.py
@@ -32,19 +32,22 @@
         )
 
 
-def attend_chunk(q3, kvbuf, limits, m_sc, l_sc, acc_sc, s, tok):
+def attend_chunk(q3, kvbuf, limits, m_sc, l_sc, acc_sc, lo, tok):
     kv_heads = q3.shape[0]
     width = kv_heads * HEAD_SIZE
     scale = HEAD_SIZE ** (-0.5)
-    lo, n = s * NEIGH * tok, NEIGH * tok
+    n = len(limits) * tok
     lane = lax.broadcasted_iota(jnp.int32, (1, n), 1)
     block = lane // tok
-    limit = jnp.full((1, n), limits[NEIGH - 1], jnp.int32)
-    for o in range(NEIGH - 2, -1, -1):
+    limit = jnp.full((1, n), limits[-1], jnp.int32)
+    for o in range(len(limits) - 2, -1, -1):
         limit = jnp.where(block == o, limits[o], limit)
     live = (lane % tok) < limit
-    for h in range(kv_heads):
-        kh = kvbuf[lo:lo + n, h * HEAD_SIZE:(h + 1) * HEAD_SIZE]
+
+    def head(h, carry):
+        kc = pl.multiple_of(h * HEAD_SIZE, HEAD_SIZE)
+        vc = pl.multiple_of(width + h * HEAD_SIZE, HEAD_SIZE)
+        kh = kvbuf[pl.ds(lo, n), pl.ds(kc, HEAD_SIZE)]
         sc = lax.dot_general(q3[h], kh, (((1,), (1,)), ((), ())), preferred_element_type=jnp.float32)
         sc = jnp.where(live, sc * scale, -1e30)
         m_old = m_sc[h]
@@ -52,9 +55,12 @@
         p = jnp.where(live, jnp.exp(sc - m_new), 0.0)
         fade = jnp.exp(m_old - m_new)
         l_sc[h] = l_sc[h] * fade + jnp.sum(p, axis=1, keepdims=True)
-        vh = kvbuf[lo:lo + n, width + h * HEAD_SIZE:width + (h + 1) * HEAD_SIZE]
+        vh = kvbuf[pl.ds(lo, n), pl.ds(vc, HEAD_SIZE)]
         acc_sc[h] = acc_sc[h] * fade + jnp.dot(p.astype(jnp.bfloat16), vh, preferred_element_type=jnp.float32)
         m_sc[h] = m_new
+        return carry
+
+    lax.fori_loop(0, kv_heads, head, 0)
 
 
 def attend_finish(own_count, l_sc, acc_sc, o_ref, groups, tok):
@@ -224,7 +230,7 @@
         @pl.when(c == cc)
         def _():
             order = [cc] + sorted(range(cc), key=lambda s: (ring_gap(s, cc), -s))
-            for s in order:
+            for s in order[:-1] if cc > 0 else []:
                 for o in range(1, NEIGH):
                     dy, dx = OFFSETS[o]
                     done = inside(o)
@@ -236,7 +242,24 @@
                             src_ref=kv_ref, dst_ref=slot(s, o), send_sem=send_sem.at[0],
                             recv_sem=recv_sem.at[s * NEIGH + o],
                             device_id=(c, i + dy, j + dx), device_id_type=mesh_id).wait_recv()
-                attend_chunk(q3, kvbuf, window_limits(s), m_sc, l_sc, acc_sc, s, tok)
+                attend_chunk(q3, kvbuf, window_limits(s), m_sc, l_sc, acc_sc, s * NEIGH * tok, tok)
+            s = order[-1]
+            limits = window_limits(s)
+            attend_chunk(q3, kvbuf, limits[:1], m_sc, l_sc, acc_sc, s * NEIGH * tok, tok)
+            for o in range(1, NEIGH):
+                dy, dx = OFFSETS[o]
+                done = inside(o)
+                if lifted and s == cc and o in (3, 4):
+                    done = done & jnp.logical_not(is_a if o == 4 else is_b)
+                @pl.when(done)
+                def _():
+                    pltpu.make_async_remote_copy(
+                        src_ref=kv_ref, dst_ref=slot(s, o), send_sem=send_sem.at[0],
+                        recv_sem=recv_sem.at[s * NEIGH + o],
+                        device_id=(c, i + dy, j + dx), device_id_type=mesh_id).wait_recv()
+                @pl.when(inside(o))
+                def _():
+                    attend_chunk(q3, kvbuf, limits[o:o + 1], m_sc, l_sc, acc_sc, (s * NEIGH + o) * tok, tok)
 
     for cc in range(spans):
         @pl.when(c == cc)

time: 46.7 us -> 52.7 us (1.13)
  Pallas kernels: 44.7 us -> 50.7 us
    pallas_call x1, Pallas kernels: 44.7 us -> 50.7 us  [window_attend(): pl.pallas_call(kernel, out_shape=jax.ShapeDtypeStruct((tok, qw), q.dtype)...]
where the time goes in v10:
time: 52.7 us; the launch traced here: 52.5 us
  Pallas kernels  50.7 us (96%)
  local copies, waits for them, and re-layouts  1.77 us (3%)
    pallas_call x1, Pallas kernels, window_attend(): pl.pallas_call(kernel, out_shape=jax.ShapeDtypeStruct((tok, qw), q.dtype)...  50.7 us
    unnamed x1, local copies, waits for them, and re-layouts  1.77 us

profile of v10, /device:TPU:95, one launch (start us, length us, event | category | flops | bytes accessed | tf_op | source)
XLA Modules:
  0.0 52.5 jit_solution(4104985376514630687)
XLA Ops:
  0.0 50.7 %shard_map.55 = bf16[128,1536]{1,0:T(8,128)(2,1)} custom-call(bf16[128,1536]{1,0:T(8,128)(2,1)} %bitcast.4, bf16[128,1024]{1,0:T(8,128)(2,1)} %bitcast.5, s32[4,8,8]{2,1,0:T(8,128)} %refs_2_.1, s32[1,1,1,5]{3,2,1,0:T(1,128)} %refs_3_.1, s32[4,4]{1,0:T(4,128)} %refs_4_.1), custom_call_target="tpu_custom_call" | custom-call | flops 2013265920 | bytes 6029312 | tf_op jit(solution)/shard_map/pallas_call | solution.py:290
  50.7 1.8 %copy.7 = bf16[1,1,1,128,1536]{4,3,2,1,0:T(8,128)(2,1)} copy(bf16[1,1,1,128,1536]{4,3,2,1,0:T(8,128)(2,1)} %bitcast.3) | data formatting | bytes 786432

commit v11 on v9

--- a/solution.py
+++ b/solution.py
@@ -32,15 +32,15 @@
         )
 
 
-def attend_chunk(q3, kvbuf, limits, m_sc, l_sc, acc_sc, s, tok):
+def attend_chunk(q3, kvbuf, limits, m_sc, l_sc, acc_sc, lo, tok):
     kv_heads = q3.shape[0]
     width = kv_heads * HEAD_SIZE
     scale = HEAD_SIZE ** (-0.5)
-    lo, n = s * NEIGH * tok, NEIGH * tok
+    n = len(limits) * tok
     lane = lax.broadcasted_iota(jnp.int32, (1, n), 1)
     block = lane // tok
-    limit = jnp.full((1, n), limits[NEIGH - 1], jnp.int32)
-    for o in range(NEIGH - 2, -1, -1):
+    limit = jnp.full((1, n), limits[-1], jnp.int32)
+    for o in range(len(limits) - 2, -1, -1):
         limit = jnp.where(block == o, limits[o], limit)
     live = (lane % tok) < limit
     for h in range(kv_heads):
@@ -224,7 +224,8 @@
         @pl.when(c == cc)
         def _():
             order = [cc] + sorted(range(cc), key=lambda s: (ring_gap(s, cc), -s))
-            for s in order:
+            split = cc == spans - 1 and cc > 0
+            for s in order[:-1] if split else order:
                 for o in range(1, NEIGH):
                     dy, dx = OFFSETS[o]
                     done = inside(o)
@@ -236,7 +237,20 @@
                             src_ref=kv_ref, dst_ref=slot(s, o), send_sem=send_sem.at[0],
                             recv_sem=recv_sem.at[s * NEIGH + o],
                             device_id=(c, i + dy, j + dx), device_id_type=mesh_id).wait_recv()
-                attend_chunk(q3, kvbuf, window_limits(s), m_sc, l_sc, acc_sc, s, tok)
+                attend_chunk(q3, kvbuf, window_limits(s), m_sc, l_sc, acc_sc, s * NEIGH * tok, tok)
+            if split:
+                s = order[-1]
+                limits = window_limits(s)
+                attend_chunk(q3, kvbuf, limits[:1], m_sc, l_sc, acc_sc, s * NEIGH * tok, tok)
+                for o in range(1, NEIGH):
+                    dy, dx = OFFSETS[o]
+                    @pl.when(inside(o))
+                    def _():
+                        pltpu.make_async_remote_copy(
+                            src_ref=kv_ref, dst_ref=slot(s, o), send_sem=send_sem.at[0],
+                            recv_sem=recv_sem.at[s * NEIGH + o],
+                            device_id=(c, i + dy, j + dx), device_id_type=mesh_id).wait_recv()
+                        attend_chunk(q3, kvbuf, limits[o:o + 1], m_sc, l_sc, acc_sc, (s * NEIGH + o) * tok, tok)
 
     for cc in range(spans):
         @pl.when(c == cc)

time: 46.7 us -> 53.4 us (1.14)
  Pallas kernels: 44.7 us -> 51.4 us
    pallas_call x1, Pallas kernels: 44.7 us -> 51.4 us  [window_attend(): pl.pallas_call(kernel, out_shape=jax.ShapeDtypeStruct((tok, qw), q.dtype)...]
where the time goes in v11:
time: 53.4 us; the launch traced here: 53.2 us
  Pallas kernels  51.4 us (96%)
  local copies, waits for them, and re-layouts  1.77 us (3%)
    pallas_call x1, Pallas kernels, window_attend(): pl.pallas_call(kernel, out_shape=jax.ShapeDtypeStruct((tok, qw), q.dtype)...  51.4 us
    unnamed x1, local copies, waits for them, and re-layouts  1.77 us

profile of v11, /device:TPU:95, one launch (start us, length us, event | category | flops | bytes accessed | tf_op | source)
XLA Modules:
  0.0 53.2 jit_solution(2158198263101263068)
XLA Ops:
  0.0 51.4 %shard_map.55 = bf16[128,1536]{1,0:T(8,128)(2,1)} custom-call(bf16[128,1536]{1,0:T(8,128)(2,1)} %bitcast.4, bf16[128,1024]{1,0:T(8,128)(2,1)} %bitcast.5, s32[4,8,8]{2,1,0:T(8,128)} %refs_2_.1, s32[1,1,1,5]{3,2,1,0:T(1,128)} %refs_3_.1, s32[4,4]{1,0:T(4,128)} %refs_4_.1), custom_call_target="tpu_custom_call" | custom-call | flops 2013265920 | bytes 6029312 | tf_op jit(solution)/shard_map/pallas_call | solution.py:281
  51.4 1.8 %copy.7 = bf16[1,1,1,128,1536]{4,3,2,1,0:T(8,128)(2,1)} copy(bf16[1,1,1,128,1536]{4,3,2,1,0:T(8,128)(2,1)} %bitcast.3) | data formatting | bytes 786432

commit v12 on v9

--- a/solution.py
+++ b/solution.py
@@ -196,23 +196,8 @@
     def ring_gap(a, b):
         return min((a - b) % spans, (b - a) % spans)
 
-    for cc in range(spans):
-        @pl.when(c == cc)
-        def _():
-            for s in sorted(range(cc), key=lambda s: (ring_gap(s, cc), -s)):
-                pltpu.make_async_remote_copy(
-                    src_ref=kv_ref, dst_ref=slot(s, 0), send_sem=send_sem.at[s], recv_sem=recv_sem.at[s * NEIGH],
-                    device_id=(s, i, j), device_id_type=mesh_id).wait_recv()
-                for d in range(1, NEIGH):
-                    send_side(s, d, slot(s, 0))
-
-    for s in range(spans):
-        @pl.when(s > c)
-        def _():
-            up_copy(s).wait_send()
     own.wait()
     q_load.wait()
-
     kv_heads = q3.shape[0]
     groups = q_ref.shape[1] // (kv_heads * HEAD_SIZE)
     load_queries(q_ref, q3, kv_heads, groups)
@@ -220,11 +205,43 @@
     l_sc[...] = jnp.zeros(l_sc.shape, jnp.float32)
     acc_sc[...] = jnp.zeros(acc_sc.shape, jnp.float32)
 
+    def own_group(cc):
+        s = cc
+        for o in range(1, NEIGH):
+            dy, dx = OFFSETS[o]
+            done = inside(o)
+            if lifted and o in (3, 4):
+                done = done & jnp.logical_not(is_a if o == 4 else is_b)
+            @pl.when(done)
+            def _():
+                pltpu.make_async_remote_copy(
+                    src_ref=kv_ref, dst_ref=slot(s, o), send_sem=send_sem.at[0],
+                    recv_sem=recv_sem.at[s * NEIGH + o],
+                    device_id=(c, i + dy, j + dx), device_id_type=mesh_id).wait_recv()
+        attend_chunk(q3, kvbuf, window_limits(s), m_sc, l_sc, acc_sc, s, tok)
+
     for cc in range(spans):
         @pl.when(c == cc)
         def _():
+            for n, s in enumerate(sorted(range(cc), key=lambda s: (ring_gap(s, cc), -s))):
+                if cc >= 2 and n == cc - 1:
+                    own_group(cc)
+                pltpu.make_async_remote_copy(
+                    src_ref=kv_ref, dst_ref=slot(s, 0), send_sem=send_sem.at[s], recv_sem=recv_sem.at[s * NEIGH],
+                    device_id=(s, i, j), device_id_type=mesh_id).wait_recv()
+                for d in range(1, NEIGH):
+                    send_side(s, d, slot(s, 0))
+
+    for s in range(spans):
+        @pl.when(s > c)
+        def _():
+            up_copy(s).wait_send()
+
+    for cc in range(spans):
+        @pl.when(c == cc)
+        def _():
             order = [cc] + sorted(range(cc), key=lambda s: (ring_gap(s, cc), -s))
-            for s in order:
+            for s in order[1:] if cc >= 2 else order:
                 for o in range(1, NEIGH):
                     dy, dx = OFFSETS[o]
                     done = inside(o)

time: 46.7 us -> 45.9 us (0.983)
  Pallas kernels: 44.7 us -> 43.9 us
    pallas_call x1, Pallas kernels: 44.7 us -> 43.9 us  [window_attend(): pl.pallas_call(kernel, out_shape=jax.ShapeDtypeStruct((tok, qw), q.dtype)...]
where the time goes in v12:
time: 45.9 us; the launch traced here: 45.7 us
  Pallas kernels  43.9 us (96%)
  local copies, waits for them, and re-layouts  1.77 us (4%)
    pallas_call x1, Pallas kernels, window_attend(): pl.pallas_call(kernel, out_shape=jax.ShapeDtypeStruct((tok, qw), q.dtype)...  43.9 us
    unnamed x1, local copies, waits for them, and re-layouts  1.77 us

profile of v12, /device:TPU:95, one launch (start us, length us, event | category | flops | bytes accessed | tf_op | source)
XLA Modules:
  0.0 45.7 jit_solution(4730234224727846550)
XLA Ops:
  0.0 43.9 %shard_map.55 = bf16[128,1536]{1,0:T(8,128)(2,1)} custom-call(bf16[128,1536]{1,0:T(8,128)(2,1)} %bitcast.4, bf16[128,1024]{1,0:T(8,128)(2,1)} %bitcast.5, s32[4,8,8]{2,1,0:T(8,128)} %refs_2_.1, s32[1,1,1,5]{3,2,1,0:T(1,128)} %refs_3_.1, s32[4,4]{1,0:T(4,128)} %refs_4_.1), custom_call_target="tpu_custom_call" | custom-call | flops 2013265920 | bytes 6029312 | tf_op jit(solution)/shard_map/pallas_call | solution.py:284
  43.9 1.8 %copy.7 = bf16[1,1,1,128,1536]{4,3,2,1,0:T(8,128)(2,1)} copy(bf16[1,1,1,128,1536]{4,3,2,1,0:T(8,128)(2,1)} %bitcast.3) | data formatting | bytes 786432

commit v13 on v12

--- a/solution.py
+++ b/solution.py
@@ -150,7 +150,7 @@
     q_load = pltpu.make_async_copy(q_hbm, q_ref, local_sem.at[1])
     q_load.start()
 
-    for s in range(spans):
+    for s in reversed(range(spans)):
         @pl.when(s > c)
         def _():
             up_copy(s).start()

time: 45.9 us -> 45.8 us (level)
  no operation moved by 1% of the time
where the time goes in v13:
time: 45.8 us; the launch traced here: 45.6 us
  Pallas kernels  43.8 us (96%)
  local copies, waits for them, and re-layouts  1.77 us (4%)
    pallas_call x1, Pallas kernels, window_attend(): pl.pallas_call(kernel, out_shape=jax.ShapeDtypeStruct((tok, qw), q.dtype)...  43.8 us
    unnamed x1, local copies, waits for them, and re-layouts  1.77 us

profile of v13, /device:TPU:95, one launch (start us, length us, event | category | flops | bytes accessed | tf_op | source)
XLA Modules:
  0.0 45.6 jit_solution(10519199377349568605)
XLA Ops:
  0.0 43.8 %shard_map.55 = bf16[128,1536]{1,0:T(8,128)(2,1)} custom-call(bf16[128,1536]{1,0:T(8,128)(2,1)} %bitcast.4, bf16[128,1024]{1,0:T(8,128)(2,1)} %bitcast.5, s32[4,8,8]{2,1,0:T(8,128)} %refs_2_.1, s32[1,1,1,5]{3,2,1,0:T(1,128)} %refs_3_.1, s32[4,4]{1,0:T(4,128)} %refs_4_.1), custom_call_target="tpu_custom_call" | custom-call | flops 2013265920 | bytes 6029312 | tf_op jit(solution)/shard_map/pallas_call | solution.py:284
  43.8 1.8 %copy.7 = bf16[1,1,1,128,1536]{4,3,2,1,0:T(8,128)(2,1)} copy(bf16[1,1,1,128,1536]{4,3,2,1,0:T(8,128)(2,1)} %bitcast.3) | data formatting | bytes 786432

commit v14 on v13

--- a/solution.py
+++ b/solution.py
@@ -179,7 +179,7 @@
                             src_ref=kv_ref, dst_ref=slot(s, o), send_sem=send_sem.at[0],
                             recv_sem=recv_sem.at[s * NEIGH + o],
                             device_id=(c, i + dy, j + dx), device_id_type=mesh_id).wait_recv()
-                for s in range(spans):
+                for s in reversed(range(spans)):
                     @pl.when(s > c)
                     def _():
                         lift_copy(s, o).start()

time: 45.8 us -> 45.8 us (level)
  no operation moved by 1% of the time
where the time goes in v14:
time: 45.8 us; the launch traced here: 45.6 us
  Pallas kernels  43.8 us (96%)
  local copies, waits for them, and re-layouts  1.77 us (4%)
    pallas_call x1, Pallas kernels, window_attend(): pl.pallas_call(kernel, out_shape=jax.ShapeDtypeStruct((tok, qw), q.dtype)...  43.8 us
    unnamed x1, local copies, waits for them, and re-layouts  1.77 us

profile of v14, /device:TPU:95, one launch (start us, length us, event | category | flops | bytes accessed | tf_op | source)
XLA Modules:
  0.0 45.6 jit_solution(11042520843572350943)
XLA Ops:
  0.0 43.8 %shard_map.55 = bf16[128,1536]{1,0:T(8,128)(2,1)} custom-call(bf16[128,1536]{1,0:T(8,128)(2,1)} %bitcast.4, bf16[128,1024]{1,0:T(8,128)(2,1)} %bitcast.5, s32[4,8,8]{2,1,0:T(8,128)} %refs_2_.1, s32[1,1,1,5]{3,2,1,0:T(1,128)} %refs_3_.1, s32[4,4]{1,0:T(4,128)} %refs_4_.1), custom_call_target="tpu_custom_call" | custom-call | flops 2013265920 | bytes 6029312 | tf_op jit(solution)/shard_map/pallas_call | solution.py:284
  43.8 1.8 %copy.7 = bf16[1,1,1,128,1536]{4,3,2,1,0:T(8,128)(2,1)} copy(bf16[1,1,1,128,1536]{4,3,2,1,0:T(8,128)(2,1)} %bitcast.3) | data formatting | bytes 786432

commit v15 on v13

--- a/solution.py
+++ b/solution.py
@@ -147,6 +147,13 @@
             cp = side_copy(s, d, src)
             cp.wait_send() if wait else cp.start()
 
+    def send_all(s, src, own=False):
+        for parity, dirs in ((0, (1, 3, 4, 2)), (1, (2, 3, 4, 1))):
+            @pl.when(i % 2 == parity)
+            def _():
+                for d in dirs:
+                    send_side(s, d, src, own=own)
+
     q_load = pltpu.make_async_copy(q_hbm, q_ref, local_sem.at[1])
     q_load.start()
 
@@ -158,8 +165,7 @@
     for s in range(spans):
         @pl.when(s == c)
         def _():
-            for d in range(1, NEIGH):
-                send_side(s, d, kv_ref, own=True)
+            send_all(s, kv_ref, own=True)
 
     own = pltpu.make_async_copy(kv_ref, slot(0, 0), local_sem.at[0])
     for s in range(spans):
@@ -229,8 +235,7 @@
                 pltpu.make_async_remote_copy(
                     src_ref=kv_ref, dst_ref=slot(s, 0), send_sem=send_sem.at[s], recv_sem=recv_sem.at[s * NEIGH],
                     device_id=(s, i, j), device_id_type=mesh_id).wait_recv()
-                for d in range(1, NEIGH):
-                    send_side(s, d, slot(s, 0))
+                send_all(s, slot(s, 0))
 
     for s in range(spans):
         @pl.when(s > c)

time: 45.8 us -> 45.8 us (level)
  no operation moved by 1% of the time
where the time goes in v15:
time: 45.8 us; the launch traced here: 45.6 us
  Pallas kernels  43.8 us (96%)
  local copies, waits for them, and re-layouts  1.77 us (4%)
    pallas_call x1, Pallas kernels, window_attend(): pl.pallas_call(kernel, out_shape=jax.ShapeDtypeStruct((tok, qw), q.dtype)...  43.8 us
    unnamed x1, local copies, waits for them, and re-layouts  1.77 us

profile of v15, /device:TPU:95, one launch (start us, length us, event | category | flops | bytes accessed | tf_op | source)
XLA Modules:
  0.0 45.6 jit_solution(12249007497914717209)
XLA Ops:
  0.0 43.8 %shard_map.55 = bf16[128,1536]{1,0:T(8,128)(2,1)} custom-call(bf16[128,1536]{1,0:T(8,128)(2,1)} %bitcast.4, bf16[128,1024]{1,0:T(8,128)(2,1)} %bitcast.5, s32[4,8,8]{2,1,0:T(8,128)} %refs_2_.1, s32[1,1,1,5]{3,2,1,0:T(1,128)} %refs_3_.1, s32[4,4]{1,0:T(4,128)} %refs_4_.1), custom_call_target="tpu_custom_call" | custom-call | flops 2013265920 | bytes 6029312 | tf_op jit(solution)/shard_map/pallas_call | solution.py:289
  43.8 1.8 %copy.7 = bf16[1,1,1,128,1536]{4,3,2,1,0:T(8,128)(2,1)} copy(bf16[1,1,1,128,1536]{4,3,2,1,0:T(8,128)(2,1)} %bitcast.3) | data formatting | bytes 786432
